TPU v7x, 128 devices: a whole 4x4x4 slice. The times are simulated.
128 devices in a mesh: rep: 32 (over y, z, x_lo), grp: 4 (over x_hi, core).
Axes of the slice: x: 4 (x_hi: 2, x_lo: 2; x = x_hi * 2 + x_lo), y: 4, z: 4, core: 2. Of those that a mesh axis runs over, the one named last changes fastest.
Arguments:
- tokens: bfloat16 [64, 1024, 768], P('rep', 'grp'), may hold values from -6 to 6
- segment: int32 [64, 1024], P('rep'), may hold values from 0 to 1, as said below
- piece_start: int32 [64, 1024], P('rep'), may hold values from 0 to 1023, as said below
- w_query: bfloat16 [768, 768], P('grp'), may hold values from -0.21875 to 0.21875
- w_key: bfloat16 [768, 768], P('grp'), may hold values from -0.21875 to 0.21875
- w_value: bfloat16 [768, 768], P('grp'), may hold values from -0.21875 to 0.21875
- w_out: bfloat16 [768, 768], P('grp'), may hold values from -3.5 to 3.5
- w_gate: bfloat16 [768, 3072], P('grp'), may hold values from -0.21875 to 0.21875
- w_up: bfloat16 [768, 3072], P('grp'), may hold values from -0.21875 to 0.21875
- w_down: bfloat16 [3072, 768], P('grp'), may hold values from -0.109375 to 0.109375
- cotangent: bfloat16 [64, 1024, 768], P('rep', 'grp'), may hold values from -6 to 6
Outputs:
- output: bfloat16 [64, 1024, 768], P('rep', 'grp')
- grad_tokens: bfloat16 [64, 1024, 768], P('rep', 'grp')
- grad_query: float32 [768, 768], P('grp')
- grad_key: float32 [768, 768], P('grp')
- grad_value: float32 [768, 768], P('grp')
- grad_out: float32 [768, 768], P('grp')
- grad_gate: float32 [768, 3072], P('grp')
- grad_up: float32 [768, 3072], P('grp')
- grad_down: float32 [3072, 768], P('grp')
Inputs may be any that keep to these rules, and one draw needn't show every extreme that they name: `segment`: along a sequence the numbers start at 0, never fall, rise by one at a time, and rise only at the first position of a picture piece. `piece_start`: each sequence holds 2 picture pieces of 256 positions, the k-th lying within positions k * (512) to (k + 1) * 512 - 1; a piece's positions hold its first position, all other positions their own.
All inputs are finite; a program needn't handle non-finite values.
Results may differ from a plain program's by a relative error of at most 0.029.
Values may be sent and summed in bfloat16 or wider, within the bound.
No kernel may reach another device: no remote copies, remote signals or barrier semaphores. Data moves between devices by JAX's collectives and lax.ppermute only.
A program may use at most 256 MiB of HBM per device.

v0:
```python
import jax
import jax.numpy as jnp
from jax import lax
from jax.sharding import Mesh
from jax.sharding import PartitionSpec as P

HEADS = 12
HDIM = 64
REP = ("y", "z", "xl")
GRP = ("xh", "c")


def layer_norm(hidden):
    centred = hidden - jnp.mean(hidden, axis=-1, keepdims=True)
    spread = jnp.mean(centred * centred, axis=-1, keepdims=True)
    return centred * lax.rsqrt(spread + 1e-05)


def rotate(heads, cosine, sine):
    half = heads.shape[-1] // 2
    first = heads[..., :half]
    second = heads[..., half:]
    return jnp.concatenate(
        [first * cosine - second * sine, second * cosine + first * sine], axis=-1
    )


def gated(gate, upper):
    return gate / (1.0 + jnp.exp(-gate)) * upper


def matmul(left, right):
    return jnp.dot(left, right, preferred_element_type=jnp.float32)


def contract_rows(left, right):
    return lax.dot_general(
        left, right, (((0,), (0,)), ((), ())), preferred_element_type=jnp.float32
    )


def contract_cols(left, right):
    return lax.dot_general(
        left, right, (((1,), (1,)), ((), ())), preferred_element_type=jnp.float32
    )


def shift(x, axis, n, step):
    return lax.ppermute(x, axis, [(i, (i + step) % n) for i in range(n)])


def place(buf, piece, index, dim):
    start = [0] * buf.ndim
    start[dim] = index * piece.shape[dim]
    return lax.dynamic_update_slice(buf, piece, start)


def ring_gather(piece, axis, n, dim):
    if n == 1:
        return piece
    me = lax.axis_index(axis)
    shape = list(piece.shape)
    shape[dim] *= n
    buf = place(jnp.zeros(shape, piece.dtype), piece, me, dim)
    if n == 2:
        return place(buf, shift(piece, axis, 2, 1), 1 - me, dim)
    back = piece
    ahead = piece
    for step in range(1, n // 2 + 1):
        if step < n - step:
            back = shift(back, axis, n, 1)
            ahead = shift(ahead, axis, n, -1)
            buf = place(buf, back, (me - step) % n, dim)
            buf = place(buf, ahead, (me + step) % n, dim)
        else:
            half = piece.shape[dim] // 2
            first = shift(lax.slice_in_dim(back, 0, half, axis=dim), axis, n, 1)
            second = shift(lax.slice_in_dim(ahead, half, piece.shape[dim], axis=dim), axis, n, -1)
            buf = place(buf, jnp.concatenate([first, second], axis=dim), (me + step) % n, dim)
    return buf


def ring_reduce(x, axis, n, dim, hdim):
    if n == 1:
        return x
    me = lax.axis_index(axis)
    size = x.shape[dim] // n

    def chunk(k, part):
        return lax.dynamic_slice_in_dim(part, k * size, size, axis=dim)

    if n == 2:
        sent = shift(chunk(1 - me, x).astype(jnp.bfloat16), axis, 2, 1)
        return chunk(me, x) + sent.astype(jnp.float32)
    half = x.shape[hdim] // 2
    parts = []
    for direction, lo, hi in ((1, 0, half), (-1, half, x.shape[hdim])):
        part = lax.slice_in_dim(x, lo, hi, axis=hdim)
        acc = chunk((me - direction) % n, part)
        for step in range(n - 1):
            got = shift(acc.astype(jnp.bfloat16), axis, n, direction)
            acc = got.astype(jnp.float32) + chunk((me - direction * (step + 2)) % n, part)
        parts.append(acc)
    return jnp.concatenate(parts, axis=hdim)


def cross(x):
    return lax.ppermute(x, ("xl", "xh"), [(i, 3 - i) for i in range(4)])


def swap_core(x):
    return lax.ppermute(x, "c", [(0, 1), (1, 0)])


def absolute(parts, rows):
    g = lax.axis_index("xh") * 2 + lax.axis_index("c")
    buf = jnp.zeros((4 * rows,) + parts[0].shape[1:], parts[0].dtype)
    for j, part in enumerate(parts):
        buf = place(buf, part, jnp.bitwise_xor(g, j), 0)
    return buf


def gather_group(own, axis, n):
    size = own.shape[0] // n
    me = lax.axis_index(axis)
    mine = lax.dynamic_slice_in_dim(own, me * size, size, axis=0)
    other = ring_gather(cross(mine), axis, n, 0)
    partner = swap_core(jnp.concatenate([own, other]))
    rows = own.shape[0]
    return [own, partner[:rows], other, partner[rows:]]


def gather_weights(shards, sizes):
    w_query, w_key, w_value, w_out, w_gate, w_up, w_down = shards
    first = jnp.concatenate([w_query, w_key, w_value, w_out, w_down])
    second = jnp.concatenate([w_gate, w_up])
    first_parts = gather_group(first, "y", sizes["y"])
    second_parts = gather_group(second, "z", sizes["z"])
    out = []
    start = 0
    for s in (w_query, w_key, w_value, w_out, w_down):
        rows = s.shape[0]
        out.append(absolute([p[start:start + rows] for p in first_parts], rows))
        start += rows
    start = 0
    for s in (w_gate, w_up):
        rows = s.shape[0]
        out.append(absolute([p[start:start + rows] for p in second_parts], rows))
        start += rows
    q, k, v, o, d, gt, up = out
    return q, k, v, o, gt, up, d


def reduce_group(grads, axes, sizes):
    g = lax.axis_index("xh") * 2 + lax.axis_index("c")
    xl = lax.axis_index("xl")

    def shard(w, j):
        rows = w.shape[0] // 4
        return lax.dynamic_slice_in_dim(w, jnp.bitwise_xor(g, j) * rows, rows, axis=0)

    send = jnp.concatenate([shard(w, 1) for w in grads] + [shard(w, 3) for w in grads])
    got = swap_core(send.astype(jnp.bfloat16)).astype(jnp.float32)
    total = got.shape[0] // 2
    own = jnp.concatenate([shard(w, 0) for w in grads]) + got[:total]
    oth = jnp.concatenate([shard(w, 2) for w in grads]) + got[total:]
    pair = jnp.stack([own, oth])
    for axis, dim, hdim in axes:
        pair = ring_reduce(pair, axis, sizes[axis], dim, hdim)
    size = pair.shape[2] // 2
    own_keep = lax.dynamic_slice_in_dim(pair[0], xl * size, size, axis=1)
    own_send = lax.dynamic_slice_in_dim(pair[0], (1 - xl) * size, size, axis=1)
    oth_keep = lax.dynamic_slice_in_dim(pair[1], (1 - xl) * size, size, axis=1)
    oth_send = lax.dynamic_slice_in_dim(pair[1], xl * size, size, axis=1)
    got = lax.ppermute(
        jnp.stack([own_send, oth_send]).astype(jnp.bfloat16), "xl", [(0, 1), (1, 0)]
    ).astype(jnp.float32)
    mine = own_keep + got[0] + cross((oth_keep + got[1]).astype(jnp.bfloat16)).astype(jnp.float32)
    full = ring_gather(mine.astype(jnp.bfloat16), "xl", 2, 1)
    for axis, dim, _ in reversed(axes):
        full = ring_gather(full, axis, sizes[axis], dim - 1)
    out = []
    start = 0
    for w in grads:
        rows = w.shape[0] // 4
        out.append(full[start:start + rows].astype(jnp.float32))
        start += rows
    return out


def to_sequence(x):
    xh = lax.axis_index("xh")
    c = lax.axis_index("c")
    first = lax.ppermute(lax.dynamic_index_in_dim(x, c, 0, False), GRP, [(0, 0), (1, 2), (2, 1), (3, 3)])
    second = lax.ppermute(lax.dynamic_index_in_dim(x, 1 - c, 0, False), GRP, [(0, 2), (1, 0), (2, 3), (3, 1)])
    return jnp.where(xh == 0, jnp.concatenate([first, second]), jnp.concatenate([second, first]))


def from_sequence(x):
    xh = lax.axis_index("xh")
    c = lax.axis_index("c")
    length = x.shape[0] // 2
    first = jnp.where(xh == 0, x[:length], x[length:])
    second = jnp.where(xh == 0, x[length:], x[:length])
    first = lax.ppermute(first, GRP, [(0, 0), (1, 2), (2, 1), (3, 3)])
    second = lax.ppermute(second, GRP, [(2, 0), (0, 1), (3, 2), (1, 3)])
    return jnp.where(c == 0, jnp.stack([first, second]), jnp.stack([second, first]))


def body(
    tokens, segment, piece_start, w_query, w_key, w_value, w_out, w_gate, w_up, w_down, cotangent
):
    sizes = {"y": lax.axis_size("y"), "z": lax.axis_size("z"), "xl": lax.axis_size("xl")}
    width = tokens.shape[2]
    local_length = tokens.shape[1] * 2
    full_length = segment.shape[1]
    head_count = HEADS
    head_size = HDIM
    scale = head_size ** (-0.5)
    xh = lax.axis_index("xh")
    c = lax.axis_index("c")
    first_row = c * local_length
    rows = first_row + jnp.arange(local_length, dtype=jnp.int32)
    columns = jnp.arange(full_length, dtype=jnp.int32)
    inverse = 10000.0 ** (-jnp.arange(0, head_size, 2).astype(jnp.float32) / head_size)
    angles = rows.astype(jnp.float32)[:, None] * inverse[None, :]
    cosine = jnp.cos(angles)[:, None, :]
    sine = jnp.sin(angles)[:, None, :]

    shards = (w_query, w_key, w_value, w_out, w_gate, w_up, w_down)
    query_weight, key_weight, value_weight, out_weight, gate_weight, up_weight, down_weight = (
        gather_weights(shards, sizes)
    )

    hidden = to_sequence(tokens).astype(jnp.float32)
    grad_result = to_sequence(cotangent)
    seg_row = lax.dynamic_index_in_dim(segment, xh, 0, False)
    start_row = lax.dynamic_index_in_dim(piece_start, xh, 0, False)

    def swap_halves(mine):
        other = lax.ppermute(mine, "c", [(0, 1), (1, 0)])
        return jnp.where(c == 0, jnp.concatenate([mine, other]), jnp.concatenate([other, mine]))

    normed, norm_one_back = jax.vjp(layer_norm, hidden)
    normed_low = normed.astype(jnp.bfloat16)
    query_heads = rotate(
        matmul(normed_low, query_weight).reshape(local_length, head_count, head_size),
        cosine,
        sine,
    ).astype(jnp.bfloat16)
    keys = (
        rotate(
            matmul(normed_low, key_weight).reshape(local_length, head_count, head_size),
            cosine,
            sine,
        )
        .reshape(local_length, width)
        .astype(jnp.bfloat16)
    )
    values = matmul(normed_low, value_weight).astype(jnp.bfloat16)
    both = swap_halves(jnp.concatenate([keys, values], axis=1))
    key_heads = both[:, :width].reshape(full_length, head_count, head_size)
    value_heads = both[:, width:].reshape(full_length, head_count, head_size)
    seg_local = lax.dynamic_slice_in_dim(seg_row, first_row, local_length)
    start_local = lax.dynamic_slice_in_dim(start_row, first_row, local_length)
    causal = columns[None, :] <= rows[:, None]
    same_piece = start_local[:, None] == start_row[None, :]
    allowed = (seg_local[:, None] == seg_row[None, :]) & (causal | same_piece)

    def scores_of(heads_in):
        raw = jnp.einsum("qhd,khd->hqk", heads_in, key_heads, preferred_element_type=jnp.float32)
        return jnp.where(allowed[None], raw * scale, -1e30)

    scores = scores_of(query_heads)
    highest = jnp.max(scores, axis=-1, keepdims=True)
    expd = jnp.exp(scores - highest)
    total = jnp.sum(expd, axis=-1, keepdims=True)
    log_total = highest + jnp.log(total)
    probs_low = (expd / total).astype(jnp.bfloat16)
    mixed = jnp.einsum("hqk,khd->qhd", probs_low, value_heads, preferred_element_type=jnp.float32)
    mixed_low = mixed.reshape(local_length, width).astype(jnp.bfloat16)
    after = hidden + matmul(mixed_low, out_weight)
    normed_two, norm_two_back = jax.vjp(layer_norm, after)
    normed_two_low = normed_two.astype(jnp.bfloat16)
    gate = matmul(normed_two_low, gate_weight)
    upper = matmul(normed_two_low, up_weight)
    active, gate_back = jax.vjp(gated, gate, upper)
    active_low = active.astype(jnp.bfloat16)
    result = after + matmul(active_low, down_weight)
    output = from_sequence(result.astype(jnp.bfloat16))

    grads = [None] * 7
    grads[6] = contract_rows(active_low, grad_result)
    grad_active = contract_cols(grad_result, down_weight)
    grad_gate, grad_upper = gate_back(grad_active)
    gate_low = grad_gate.astype(jnp.bfloat16)
    upper_low = grad_upper.astype(jnp.bfloat16)
    grads[4] = contract_rows(normed_two_low, gate_low)
    grads[5] = contract_rows(normed_two_low, upper_low)
    grad_normed_two = contract_cols(gate_low, gate_weight) + contract_cols(upper_low, up_weight)
    grad_after = grad_result.astype(jnp.float32) + norm_two_back(grad_normed_two)[0]
    after_low = grad_after.astype(jnp.bfloat16)
    grads[3] = contract_rows(mixed_low, after_low)
    grad_mixed = (
        contract_cols(after_low, out_weight)
        .astype(jnp.bfloat16)
        .reshape(local_length, head_count, head_size)
    )
    probs = jnp.exp(scores_of(query_heads) - log_total)
    grad_probs = jnp.einsum("qhd,khd->hqk", grad_mixed, value_heads, preferred_element_type=jnp.float32)
    inner = jnp.sum(probs * grad_probs, axis=-1, keepdims=True)
    grad_raw = (probs * (grad_probs - inner) * scale).astype(jnp.bfloat16)
    grad_query = jnp.einsum("hqk,khd->qhd", grad_raw, key_heads, preferred_element_type=jnp.float32)
    again_low = probs.astype(jnp.bfloat16)
    grad_keys = jnp.einsum(
        "hqk,qhd->khd", grad_raw, query_heads, preferred_element_type=jnp.float32
    ).reshape(full_length, width)
    grad_values = jnp.einsum(
        "hqk,qhd->khd", again_low, grad_mixed, preferred_element_type=jnp.float32
    ).reshape(full_length, width)
    grad_kv = jnp.concatenate([grad_keys, grad_values], axis=1)
    mine_kv = jnp.where(c == 0, grad_kv[:local_length], grad_kv[local_length:])
    theirs_kv = jnp.where(c == 0, grad_kv[local_length:], grad_kv[:local_length])
    own_kv = mine_kv + lax.ppermute(theirs_kv, "c", [(0, 1), (1, 0)])
    own_keys = own_kv[:, :width]
    own_values = own_kv[:, width:]
    query_low = (
        rotate(grad_query, cosine, -sine).reshape(local_length, width).astype(jnp.bfloat16)
    )
    keys_low = (
        rotate(own_keys.reshape(local_length, head_count, head_size), cosine, -sine)
        .reshape(local_length, width)
        .astype(jnp.bfloat16)
    )
    values_low = own_values.astype(jnp.bfloat16)
    grads[0] = contract_rows(normed_low, query_low)
    grads[1] = contract_rows(normed_low, keys_low)
    grads[2] = contract_rows(normed_low, values_low)
    grad_normed = (
        contract_cols(query_low, query_weight)
        + contract_cols(keys_low, key_weight)
        + contract_cols(values_low, value_weight)
    )
    grad_hidden = grad_after + norm_one_back(grad_normed)[0]
    input_grads = from_sequence(grad_hidden.astype(jnp.bfloat16))

    wide = reduce_group([grads[4], grads[5]], (("y", 1, 2), ("z", 2, 1)), sizes)
    narrow = reduce_group(
        [grads[6], grads[3], grads[0], grads[1], grads[2]], (("y", 1, 2), ("z", 1, 2)), sizes
    )
    owned = [narrow[2], narrow[3], narrow[4], narrow[1], wide[0], wide[1], narrow[0]]
    return (output, input_grads, *owned)


def solution(mesh):
    rep, grp = mesh.devices.shape
    side = int(round((rep // 2) ** 0.5))
    devices = mesh.devices.reshape(side, rep // (2 * side), 2, grp // 2, 2)
    fine = Mesh(devices, ("y", "z", "xl", "xh", "c"))
    seqs = P(REP, GRP, None)
    rows = P(GRP, None)
    placed = (seqs, P(REP, None), P(REP, None), rows, rows, rows, rows, rows, rows, rows, seqs)
    return jax.shard_map(
        body,
        mesh=fine,
        in_specs=placed,
        out_specs=(seqs, seqs, rows, rows, rows, rows, rows, rows, rows),
        check_vma=False,
    )
```

profile of v0, /device:TPU:0, one launch (start us, length us, event | category | flops | bytes accessed | tf_op | source)
XLA Modules:
  0.0 674.2 jit_solution(17173276268030057847)
XLA Ops:
  15.7 13.4 %collective-permute-done.2 = bf16[384,768]{1,0:T(8,128)(2,1)} collective-permute-done((bf16[384,768]{1,0:T(8,128)(2,1)S(1)}, bf16[384,768]{1,0:T(8,128)(2,1)}, u32[]{:S(2)}, u32[]{:S(2)}) %collective-permute-start.2) | collective-permute-done | bytes 589856 | tf_op jit(solution)/shard_map/ppermute | solution.py:108
  67.5 11.3 %collective-permute-done.11 = bf16[96,3072]{1,0:T(8,128)(2,1)S(1)} collective-permute-done((bf16[96,3072]{1,0:T(8,128)(2,1)}, bf16[96,3072]{1,0:T(8,128)(2,1)S(1)}, u32[]{:S(2)}, u32[]{:S(2)}) %collective-permute-start.11) | collective-permute-done | bytes 589856 | tf_op jit(solution)/shard_map/ppermute | solution.py:49
  82.6 5.9 collective-permute-done.13
  98.8 6.7 collective-permute-start.17
  134.7 7.8 %fusion.123 = f32[512,3072]{1,0:T(8,128)} fusion(bf16[3072,768]{1,0:T(8,128)(2,1)} %slice_dynamic-update-slice_fusion, bf16[256,768]{1,0:T(8,128)(2,1)S(1)} %collective-permute-done.18, bf16[256,768]{1,0:T(8,128)(2,1)} %collective-permute-done.17, pred[]{:T(512)S(6)} %eq.105), kind=kOutput, calls=%fused_computation.364 | convolution fusion | flops 2419458048 | bytes 11796481 | tf_op jit(solution)/shard_map/dot_general | solution.py:43
  146.1 12.6 %maximum_select_fusion = bf16[1024,1536]{1,0:T(8,128)(2,1)S(1)} fusion(bf16[512,1536]{1,0:T(8,128)(2,1)S(1)} %collective-permute-done.8, bf16[512,768]{1,0:T(8,128)(2,1)S(1)} %convolution_convert_fusion.1, bf16[512,768]{1,0:T(8,128)(2,1)S(1)} %copy-done.25, pred[]{:T(512)S(6)} %eq.104), kind=kLoop, calls=%fused_computation.56 | loop fusion | flops 20447232 | bytes 6291457 | tf_op jit(solution)/shard_map/jit(_where)/select_n | solution.py:242
  165.5 14.3 %fusion.3 = (f32[12,512]{1,0:T(8,128)S(1)}, f32[12,512,1024]{2,1,0:T(8,128)}) fusion(pred[512,1024]{1,0:T(8,128)(4,1)S(1)} %copy-done.29, bf16[1024,12,64]{0,2,1:T(8,128)(2,1)} %bitcast.121, bf16[512,12,32]{0,2,1:T(8,128)(2,1)} %get-tuple-element.65, bf16[512,12,32]{0,2,1:T(8,128)(2,1)} %get-tuple-element.64), kind=kOutput, calls=%fused_computation.9 | convolution fusion | flops 825747456 | bytes 28073984 | tf_op jit(solution)/shard_map/qhd,khd->hqk/dot_general | solution.py:271
  179.8 12.5 %fusion.2 = f32[12,512]{1,0:T(8,128)S(1)} fusion(f32[12,512,1024]{2,1,0:T(8,128)} %get-tuple-element.99, f32[12,512]{1,0:T(8,128)S(1)} %get-tuple-element.98, pred[512,1024]{1,0:T(8,128)(4,1)S(1)} %copy-done.29), kind=kLoop, calls=%fused_computation.8 | loop fusion | flops 25159680 | bytes 25739264 | tf_op jit(solution)/shard_map/reduce_sum | solution.py:277
  195.2 8.5 %fusion.34 = bf16[12,64,512]{2,1,0:T(8,128)(2,1)} fusion(bf16[1024,12,64]{0,2,1:T(8,128)(2,1)S(1)} %bitcast.112, f32[12,512,1024]{2,1,0:T(8,128)S(1)} %copy-done, f32[12,512]{1,0:T(8,128)S(1)} %fusion.2, f32[12,512]{1,0:T(8,128)S(1)} %get-tuple-element.98, pred[512,1024]{1,0:T(8,128)(4,1)S(1)} %copy-done.29), kind=kOutput, calls=%fused_computation.99 | convolution fusion | flops 837156864 | bytes 28098560 | tf_op jit(solution)/shard_map/hqk,khd->qhd/dot_general | solution.py:280
  209.2 9.2 %add_convert_fusion = (bf16[512,3072]{1,0:T(8,128)(2,1)S(1)}, bf16[512,3072]{1,0:T(8,128)(2,1)S(1)}, bf16[512,3072]{1,0:T(8,128)(2,1)}) fusion(f32[512,3072]{1,0:T(8,128)} %fusion.123, f32[512,3072]{1,0:T(8,128)S(1)} %fusion.131, bf16[512,768]{1,0:T(8,128)(2,1)S(1)} %multiply_convert_fusion.3, bf16[768,3072]{1,0:T(8,128)(2,1)S(1)} %bitcast.126), kind=kOutput, calls=%fused_computation.22 | convolution fusion | flops 2444230656 | bytes 27525120 | tf_op jit(solution)/shard_map/dot_general | solution.py:33
  221.0 5.5 fusion.140
  252.0 11.5 %fusion.133 = f32[12,512,1024]{2,1,0:T(8,128)} fusion(bf16[512,12,64]{0,2,1:T(8,128)(2,1)} %bitcast.118, bf16[1024,12,64]{0,2,1:T(8,128)(2,1)S(1)} %bitcast.113), kind=kOutput, calls=%fused_computation.372 | convolution fusion | flops 805306368 | bytes 27525120 | tf_op jit(solution)/shard_map/qhd,khd->hqk/dot_general | solution.py:310
  263.5 13.3 %fusion.4 = f32[12,64,1024]{2,1,0:T(8,128)} fusion(bf16[512,12,64]{0,2,1:T(8,128)(2,1)S(1)} %bitcast.119, f32[12,512,1024]{2,1,0:T(8,128)} %get-tuple-element.99, f32[12,512]{1,0:T(8,128)S(1)} %copy-done.62, pred[512,1024]{1,0:T(8,128)(4,1)S(1)} %copy-done.30), kind=kOutput, calls=%fused_computation.10 | convolution fusion | flops 830472192 | bytes 29646848 | tf_op jit(solution)/shard_map/hqk,qhd->khd/dot_general | solution.py:318
  276.8 54.2 %fusion.10 = f32[12,64,1024]{2,1,0:T(8,128)} fusion(f32[12,512,1024]{2,1,0:T(8,128)} %fusion.133, f32[12,512]{1,0:T(8,128)} %log_add_fusion, f32[12,512,1024]{2,1,0:T(8,128)} %get-tuple-element.99, pred[512,1024]{1,0:T(8,128)(4,1)} %fusion.27, bf16[512,12,32]{0,2,1:T(8,128)(2,1)S(1)} %copy-done.35, bf16[512,12,32]{0,2,1:T(8,128)(2,1)S(1)} %copy-done.34), kind=kOutput, calls=%fused_computation.13 | convolution fusion | flops 876092416 | bytes 54812672 | tf_op jit(solution)/shard_map/hqk,qhd->khd/dot_general | solution.py:315
  354.4 52.5 %fusion.31 = f32[512,12,64]{0,2,1:T(8,128)} fusion(bf16[1024,12,64]{0,2,1:T(8,128)(2,1)S(1)} %bitcast.122, f32[12,512,1024]{2,1,0:T(8,128)} %fusion.133, f32[12,512]{1,0:T(8,128)} %log_add_fusion, f32[12,512,1024]{2,1,0:T(8,128)} %get-tuple-element.99, pred[512,1024]{1,0:T(8,128)(4,1)} %fusion.27), kind=kOutput, calls=%fused_computation.95 | convolution fusion | flops 874519552 | bytes 54026240 | tf_op jit(solution)/shard_map/hqk,khd->qhd/dot_general | solution.py:313
  409.2 7.9 %constant_dynamic-slice_fusion = (f32[192,3072]{1,0:T(8,128)}, f32[192,3072]{1,0:T(8,128)}, f32[192,3072]{1,0:T(8,128)}, f32[192,3072]{1,0:T(8,128)}) fusion(f32[768,3072]{1,0:T(8,128)} %fusion.140, s32[]{:T(128)S(6)} %select_n.460, s32[]{:T(128)S(6)} %select_n.451, f32[768,3072]{1,0:T(8,128)} %fusion.139), kind=kLoop, calls=%fused_computation.307 | loop fusion | bytes 18874376 | tf_op jit(solution)/shard_map/dynamic_slice | solution.py:160
  458.6 11.5 %collective-permute-done.47 = bf16[2,96,1536]{2,1,0:T(8,128)(2,1)S(1)} collective-permute-done((bf16[2,96,1536]{2,1,0:T(8,128)(2,1)S(1)}, bf16[2,96,1536]{2,1,0:T(8,128)(2,1)S(1)}, u32[]{:S(2)}, u32[]{:S(2)}) %collective-permute-start.47) | collective-permute-done | bytes 589856 | tf_op jit(solution)/shard_map/ppermute | solution.py:49
  476.9 8.9 %collective-permute-done.48 = bf16[2,96,1536]{2,1,0:T(8,128)(2,1)S(1)} collective-permute-done((bf16[2,96,1536]{2,1,0:T(8,128)(2,1)S(1)}, bf16[2,96,1536]{2,1,0:T(8,128)(2,1)S(1)}, u32[]{:S(2)}, u32[]{:S(2)}) %collective-permute-start.48) | collective-permute-done | bytes 589856 | tf_op jit(solution)/shard_map/ppermute | solution.py:49
  490.4 10.3 %collective-permute-done.49 = bf16[2,96,1536]{2,1,0:T(8,128)(2,1)S(1)} collective-permute-done((bf16[2,96,1536]{2,1,0:T(8,128)(2,1)S(1)}, bf16[2,96,1536]{2,1,0:T(8,128)(2,1)S(1)}, u32[]{:S(2)}, u32[]{:S(2)}) %collective-permute-start.49) | collective-permute-done | bytes 589856 | tf_op jit(solution)/shard_map/ppermute | solution.py:49
  532.8 11.2 %fusion.19 = (f32[1,1536,768]{2,1,0:T(8,128)}, f32[1,1536,768]{2,1,0:T(8,128)}) fusion(f32[1536,768]{1,0:T(8,128)} %get-tuple-element.49, f32[3072,768]{1,0:T(8,128)} %convert_element_type.310, f32[1536,768]{1,0:T(8,128)} %get-tuple-element.50), kind=kLoop, calls=%fused_computation.33 | loop fusion | flops 2359296 | bytes 28311552 | tf_op jit(solution)/shard_map/stack | solution.py:167
  554.8 7.4 %collective-permute-done.23 = bf16[2,384,384]{2,1,0:T(8,128)(2,1)S(1)} collective-permute-done((bf16[2,384,384]{2,1,0:T(8,128)(2,1)S(1)}, bf16[2,384,384]{2,1,0:T(8,128)(2,1)S(1)}, u32[]{:S(2)}, u32[]{:S(2)}) %collective-permute-start.23) | collective-permute-done | bytes 589856 | tf_op jit(solution)/shard_map/ppermute | solution.py:49
  562.8 7.1 %collective-permute-start.63 = (bf16[96,768]{1,0:T(8,128)(2,1)S(1)}, bf16[96,768]{1,0:T(8,128)(2,1)S(1)}, u32[]{:S(2)}, u32[]{:S(2)}) collective-permute-start(bf16[96,768]{1,0:T(8,128)(2,1)S(1)} %constant_dynamic-update-slice_fusion.17), channel_id=1, source_target_pairs={{0,24},{8,0},{16,8},{24,16},{1,25},{9,1},{17,9},{25,17},{2,26},{10... | collective-permute-start | bytes 442376 | tf_op jit(solution)/shard_map/ppermute | solution.py:49
  579.5 8.1 %collective-permute-done.30 = bf16[2,384,384]{2,1,0:T(8,128)(2,1)S(1)} collective-permute-done((bf16[2,384,384]{2,1,0:T(8,128)(2,1)S(1)}, bf16[2,384,384]{2,1,0:T(8,128)(2,1)S(1)}, u32[]{:S(2)}, u32[]{:S(2)}) %collective-permute-start.30) | collective-permute-done | bytes 589856 | tf_op jit(solution)/shard_map/ppermute | solution.py:49
  654.3 5.3 collective-permute-done.43
  (511 shorter events, 354.6 us)
Async XLA Ops:
  32.2 16.7 %collective-permute-start.3 = (bf16[384,768]{1,0:T(8,128)(2,1)}, bf16[384,768]{1,0:T(8,128)(2,1)}, u32[]{:S(2)}, u32[]{:S(2)}) collective-permute-start(bf16[384,768]{1,0:T(8,128)(2,1)} %collective-permute-done.2), channel_id=1, source_target_pairs={{0,32},{32,64},{64,96},{96,0},{1,33},{33,65},{65,97},{97,1},{2,34}... | collective-permute-start | bytes 1769480 | tf_op jit(solution)/shard_map/ppermute | solution.py:49
  33.1 65.6 %collective-permute-start = (bf16[256,768]{1,0:T(8,128)(2,1)}, bf16[256,768]{1,0:T(8,128)(2,1)S(1)}, u32[]{:S(2)}, u32[]{:S(2)}) collective-permute-start(bf16[256,768]{1,0:T(8,128)(2,1)} %get-tuple-element.78), channel_id=1, source_target_pairs={{0,0},{1,2},{2,1},{3,3},{4,4},{5,6},{6,5},{7,7},{8,8},{9,10},{10,9... | collective-permute-start | bytes 1179656 | tf_op jit(solution)/shard_map/ppermute | solution.py:194
  34.8 70.8 %collective-permute-start.1 = (bf16[256,768]{1,0:T(8,128)(2,1)}, bf16[256,768]{1,0:T(8,128)(2,1)S(1)}, u32[]{:S(2)}, u32[]{:S(2)}) collective-permute-start(bf16[256,768]{1,0:T(8,128)(2,1)} %get-tuple-element.77), channel_id=1, source_target_pairs={{0,2},{1,0},{2,3},{3,1},{4,6},{5,4},{6,7},{7,5},{8,10},{9,8},{10,1... | collective-permute-start | bytes 1179656 | tf_op jit(solution)/shard_map/ppermute | solution.py:195
  38.1 22.8 %collective-permute-start.9 = (bf16[96,3072]{1,0:T(8,128)(2,1)}, bf16[96,3072]{1,0:T(8,128)(2,1)}, u32[]{:S(2)}, u32[]{:S(2)}) collective-permute-start(bf16[96,3072]{1,0:T(8,128)(2,1)} %fusion.59), channel_id=1, source_target_pairs={{0,6},{2,4},{4,2},{6,0},{1,7},{3,5},{5,3},{7,1},{8,14},{10,12},{12... | collective-permute-start | bytes 1769480 | tf_op jit(solution)/shard_map/ppermute | solution.py:108
  59.4 47.2 %collective-permute-start.7 = (bf16[3072,768]{1,0:T(8,128)(2,1)}, bf16[3072,768]{1,0:T(8,128)(2,1)}, u32[]{:S(2)}, u32[]{:S(2)}) collective-permute-start(bf16[3072,768]{1,0:T(8,128)(2,1)} %constant_dynamic-update-slice_fusion.5), channel_id=1, source_target_pairs={{0,1},{1,0},{2,3},{3,2},{4,5},{5,4},{6,7},{7,6},{8,9},{9,8},{10,11... | collective-permute-start | bytes 14155784 | tf_op jit(solution)/shard_map/ppermute | solution.py:112
  60.9 21.4 %collective-permute-start.10 = (bf16[96,3072]{1,0:T(8,128)(2,1)}, bf16[96,3072]{1,0:T(8,128)(2,1)S(1)}, u32[]{:S(2)}, u32[]{:S(2)}) collective-permute-start(bf16[96,3072]{1,0:T(8,128)(2,1)} %collective-permute-done.9), channel_id=1, source_target_pairs={{0,8},{8,16},{16,24},{24,0},{1,9},{9,17},{17,25},{25,1},{2,10},{10... | collective-permute-start | bytes 1769480 | tf_op jit(solution)/shard_map/ppermute | solution.py:49
  88.5 46.2 %collective-permute-start.18 = (bf16[256,768]{1,0:T(8,128)(2,1)}, bf16[256,768]{1,0:T(8,128)(2,1)S(1)}, u32[]{:S(2)}, u32[]{:S(2)}) collective-permute-start(bf16[256,768]{1,0:T(8,128)(2,1)} %get-tuple-element.74), channel_id=1, source_target_pairs={{0,2},{1,0},{2,3},{3,1},{4,6},{5,4},{6,7},{7,5},{8,10},{9,8},{10,1... | collective-permute-start | bytes 1179656 | tf_op jit(solution)/shard_map/ppermute | solution.py:195
  95.0 27.0 %collective-permute-start.14 = (bf16[768,3072]{1,0:T(8,128)(2,1)}, bf16[768,3072]{1,0:T(8,128)(2,1)}, u32[]{:S(2)}, u32[]{:S(2)}) collective-permute-start(bf16[768,3072]{1,0:T(8,128)(2,1)} %pad_maximum_fusion), channel_id=1, source_target_pairs={{0,1},{1,0},{2,3},{3,2},{4,5},{5,4},{6,7},{7,6},{8,9},{9,8},{10,11... | collective-permute-start | bytes 14155784 | tf_op jit(solution)/shard_map/ppermute | solution.py:112
  98.8 35.9 %collective-permute-start.17 = (bf16[256,768]{1,0:T(8,128)(2,1)}, bf16[256,768]{1,0:T(8,128)(2,1)}, u32[]{:S(2)}, u32[]{:S(2)}) collective-permute-start(bf16[256,768]{1,0:T(8,128)(2,1)} %get-tuple-element.73), channel_id=1, source_target_pairs={{0,0},{1,2},{2,1},{3,3},{4,4},{5,6},{6,5},{7,7},{8,8},{9,10},{10,9... | collective-permute-start | bytes 1179656 | tf_op jit(solution)/shard_map/ppermute | solution.py:194
  121.9 24.2 %collective-permute-start.8 = (bf16[512,1536]{1,0:T(8,128)(2,1)S(1)}, bf16[512,1536]{1,0:T(8,128)(2,1)S(1)}, u32[]{:S(2)}, u32[]{:S(2)}) collective-permute-start(bf16[512,1536]{1,0:T(8,128)(2,1)S(1)} %pad_maximum_fusion.3), channel_id=1, source_target_pairs={{0,1},{1,0},{2,3},{3,2},{4,5},{5,4},{6,7},{7,6},{8,9},{9,8},{10,11... | collective-permute-start | bytes 4718600 | tf_op jit(solution)/shard_map/ppermute | solution.py:241
  232.4 189.3 %collective-permute-start.16 = (bf16[256,768]{1,0:T(8,128)(2,1)}, bf16[256,768]{1,0:T(8,128)(2,1)}, u32[]{:S(2)}, u32[]{:S(2)}) collective-permute-start(bf16[256,768]{1,0:T(8,128)(2,1)} %get-tuple-element.76), channel_id=1, source_target_pairs={{2,0},{0,1},{3,2},{1,3},{6,4},{4,5},{7,6},{5,7},{10,8},{8,9},{11,1... | collective-permute-start | bytes 1179656 | tf_op jit(solution)/shard_map/ppermute | solution.py:206
  232.7 189.0 %collective-permute-start.15 = (bf16[256,768]{1,0:T(8,128)(2,1)}, bf16[256,768]{1,0:T(8,128)(2,1)}, u32[]{:S(2)}, u32[]{:S(2)}) collective-permute-start(bf16[256,768]{1,0:T(8,128)(2,1)} %get-tuple-element.75), channel_id=1, source_target_pairs={{0,0},{1,2},{2,1},{3,3},{4,4},{5,6},{6,5},{7,7},{8,8},{9,10},{10,9... | collective-permute-start | bytes 1179656 | tf_op jit(solution)/shard_map/ppermute | solution.py:205
  336.2 88.0 %collective-permute-start.19 = (f32[512,1536]{0,1:T(8,128)}, f32[512,1536]{0,1:T(8,128)}, u32[]{:S(2)}, u32[]{:S(2)}) collective-permute-start(f32[512,1536]{0,1:T(8,128)} %broadcast_select_fusion), channel_id=1, source_target_pairs={{0,1},{1,0},{2,3},{3,2},{4,5},{5,4},{6,7},{7,6},{8,9},{9,8},{10,11... | collective-permute-start | bytes 9437192 | tf_op jit(solution)/shard_map/ppermute | solution.py:324
  344.0 100.3 %collective-permute-start.46 = (bf16[768,3072]{1,0:T(8,128)(2,1)}, bf16[768,3072]{1,0:T(8,128)(2,1)}, u32[]{:S(2)}, u32[]{:S(2)}) collective-permute-start(bf16[768,3072]{1,0:T(8,128)(2,1)} %pad_maximum_fusion.1), channel_id=1, source_target_pairs={{0,1},{1,0},{2,3},{3,2},{4,5},{5,4},{6,7},{7,6},{8,9},{9,8},{10,11... | collective-permute-start | bytes 14155784 | tf_op jit(solution)/shard_map/ppermute | solution.py:112
  453.5 16.5 %collective-permute-start.47 = (bf16[2,96,1536]{2,1,0:T(8,128)(2,1)S(1)}, bf16[2,96,1536]{2,1,0:T(8,128)(2,1)S(1)}, u32[]{:S(2)}, u32[]{:S(2)}) collective-permute-start(bf16[2,96,1536]{2,1,0:T(8,128)(2,1)S(1)} %dynamic-slice_convert_fusion.6), channel_id=1, source_target_pairs={{0,32},{32,64},{64,96},{96,0},{1,33},{33,65},{65,97},{97,1},{2,34}... | collective-permute-start | bytes 1769480 | tf_op jit(solution)/shard_map/ppermute | solution.py:49
  458.5 70.0 %collective-permute-start.22 = (bf16[3072,768]{1,0:T(8,128)(2,1)S(1)}, bf16[3072,768]{1,0:T(8,128)(2,1)S(1)}, u32[]{:S(2)}, u32[]{:S(2)}) collective-permute-start(bf16[3072,768]{1,0:T(8,128)(2,1)S(1)} %fusion.70), channel_id=1, source_target_pairs={{0,1},{1,0},{2,3},{3,2},{4,5},{5,4},{6,7},{7,6},{8,9},{9,8},{10,11... | collective-permute-start | bytes 14155784 | tf_op jit(solution)/shard_map/ppermute | solution.py:112
  489.6 80.4 %collective-permute-start.21 = (bf16[256,768]{1,0:T(8,128)(2,1)S(1)}, bf16[256,768]{1,0:T(8,128)(2,1)S(1)}, u32[]{:S(2)}, u32[]{:S(2)}) collective-permute-start(bf16[256,768]{1,0:T(8,128)(2,1)S(1)} %get-tuple-element.72), channel_id=1, source_target_pairs={{2,0},{0,1},{3,2},{1,3},{6,4},{4,5},{7,6},{5,7},{10,8},{8,9},{11,1... | collective-permute-start | bytes 1179656 | tf_op jit(solution)/shard_map/ppermute | solution.py:206
  489.7 84.1 %collective-permute-start.20 = (bf16[256,768]{1,0:T(8,128)(2,1)S(1)}, bf16[256,768]{1,0:T(8,128)(2,1)S(1)}, u32[]{:S(2)}, u32[]{:S(2)}) collective-permute-start(bf16[256,768]{1,0:T(8,128)(2,1)S(1)} %get-tuple-element.71), channel_id=1, source_target_pairs={{0,0},{1,2},{2,1},{3,3},{4,4},{5,6},{6,5},{7,7},{8,8},{9,10},{10,9... | collective-permute-start | bytes 1179656 | tf_op jit(solution)/shard_map/ppermute | solution.py:205
  562.3 16.6 %collective-permute-start.24 = (bf16[2,384,384]{2,1,0:T(8,128)(2,1)S(1)}, bf16[2,384,384]{2,1,0:T(8,128)(2,1)S(1)}, u32[]{:S(2)}, u32[]{:S(2)}) collective-permute-start(bf16[2,384,384]{2,1,0:T(8,128)(2,1)S(1)} %add_convert_fusion.6), channel_id=1, source_target_pairs={{0,32},{32,64},{64,96},{96,0},{1,33},{33,65},{65,97},{97,1},{2,34}... | collective-permute-start | bytes 1769480 | tf_op jit(solution)/shard_map/ppermute | solution.py:49
  570.0 17.5 %collective-permute-start.30 = (bf16[2,384,384]{2,1,0:T(8,128)(2,1)S(1)}, bf16[2,384,384]{2,1,0:T(8,128)(2,1)S(1)}, u32[]{:S(2)}, u32[]{:S(2)}) collective-permute-start(bf16[2,384,384]{2,1,0:T(8,128)(2,1)S(1)} %fusion.44), channel_id=1, source_target_pairs={{0,96},{32,0},{64,32},{96,64},{1,97},{33,1},{65,33},{97,65},{2,98}... | collective-permute-start | bytes 1769480 | tf_op jit(solution)/shard_map/ppermute | solution.py:49
  574.9 16.6 %collective-permute-start.65 = (bf16[96,384]{1,0:T(8,128)(2,1)S(1)}, bf16[96,384]{1,0:T(8,128)(2,1)S(1)}, u32[]{:S(2)}, u32[]{:S(2)}) collective-permute-start(bf16[96,384]{1,0:T(8,128)(2,1)S(1)} %slice.403), channel_id=1, source_target_pairs={{0,24},{8,0},{16,8},{24,16},{1,25},{9,1},{17,9},{25,17},{2,26},{10... | collective-permute-start | bytes 221192 | tf_op jit(solution)/shard_map/ppermute | solution.py:49
  591.5 29.5 %collective-permute-start.66 = (bf16[96,3072]{1,0:T(8,128)(2,1)S(1)}, bf16[96,3072]{1,0:T(8,128)(2,1)S(1)}, u32[]{:S(2)}, u32[]{:S(2)}) collective-permute-start(bf16[96,3072]{1,0:T(8,128)(2,1)S(1)} %maximum_dynamic-update-slice_fusion.5), channel_id=1, source_target_pairs={{0,32},{32,64},{64,96},{96,0},{1,33},{33,65},{65,97},{97,1},{2,34}... | collective-permute-start | bytes 1769480 | tf_op jit(solution)/shard_map/ppermute | solution.py:49
  591.6 25.6 %collective-permute-start.67 = (bf16[96,3072]{1,0:T(8,128)(2,1)S(1)}, bf16[96,3072]{1,0:T(8,128)(2,1)S(1)}, u32[]{:S(2)}, u32[]{:S(2)}) collective-permute-start(bf16[96,3072]{1,0:T(8,128)(2,1)S(1)} %maximum_dynamic-update-slice_fusion.5), channel_id=1, source_target_pairs={{0,96},{32,0},{64,32},{96,64},{1,97},{33,1},{65,33},{97,65},{2,98}... | collective-permute-start | bytes 1769480 | tf_op jit(solution)/shard_map/ppermute | solution.py:49
  617.2 18.2 %collective-permute-start.69 = (bf16[48,3072]{1,0:T(8,128)(2,1)S(1)}, bf16[48,3072]{1,0:T(8,128)(2,1)S(1)}, u32[]{:S(2)}, u32[]{:S(2)}) collective-permute-start(bf16[48,3072]{1,0:T(8,128)(2,1)S(1)} %slice.405), channel_id=1, source_target_pairs={{0,96},{32,0},{64,32},{96,64},{1,97},{33,1},{65,33},{97,65},{2,98}... | collective-permute-start | bytes 884744 | tf_op jit(solution)/shard_map/ppermute | solution.py:49
  (128 other events, 1119.7 us)
where the time goes:
time: 684 us; the launch traced here: 674 us
  matrix products  215 us (31%)
  waiting for transfers between devices  144 us (21%)
  starting transfers between devices  114 us (17%)
  local copies, waits for them, and re-layouts  104 us (15%)
  other arithmetic  93.5 us (14%)
    ppermute x50, waiting for transfers between devices, shift(): return lax.ppermute(x, axis, [(i, (i + step) % n) for i in range(n)])  125 us
    ppermute x50, starting transfers between devices, shift(): return lax.ppermute(x, axis, [(i, (i + step) % n) for i in range(n)])  83.7 us
    dot_general x1, matrix products, body(): jnp.einsum('hqk,qhd->khd', grad_raw, query_heads, preferred_element_type=...  54.2 us
    dot_general x1, matrix products, body(): jnp.einsum('hqk,khd->qhd', grad_raw, key_heads, preferred_element_type=jn...  52.5 us
    unnamed x178, local copies, waits for them, and re-layouts  34.6 us
    dynamic_update_slice x39, local copies, waits for them, and re-layouts, place(): return lax.dynamic_update_slice(buf, piece, start)  32.6 us
    dot_general x7, matrix products, matmul(): return jnp.dot(left, right, preferred_element_type=jnp.float32)  22.9 us
    another operation x4, other arithmetic, reduce_group(): pair = jnp.stack([own, oth])  19.4 us
  transfers between devices with their start and end apart: 70, of which 37 were waited for; matrix products, arithmetic and copies ran while one was open for 43% of the time, Pallas kernels for 0%

commit v1 on v0

--- a/solution.py
+++ b/solution.py
@@ -132,23 +132,22 @@
 
 def gather_weights(shards, sizes):
     w_query, w_key, w_value, w_out, w_gate, w_up, w_down = shards
-    first = jnp.concatenate([w_query, w_key, w_value, w_out, w_down])
-    second = jnp.concatenate([w_gate, w_up])
-    first_parts = gather_group(first, "y", sizes["y"])
-    second_parts = gather_group(second, "z", sizes["z"])
+    plan = (
+        ((w_query, w_key, w_value), "y"),
+        ((w_out,), "z"),
+        ((w_gate,), "y"),
+        ((w_up,), "z"),
+        ((w_down,), "z"),
+    )
     out = []
-    start = 0
-    for s in (w_query, w_key, w_value, w_out, w_down):
-        rows = s.shape[0]
-        out.append(absolute([p[start:start + rows] for p in first_parts], rows))
-        start += rows
-    start = 0
-    for s in (w_gate, w_up):
-        rows = s.shape[0]
-        out.append(absolute([p[start:start + rows] for p in second_parts], rows))
-        start += rows
-    q, k, v, o, d, gt, up = out
-    return q, k, v, o, gt, up, d
+    for group, axis in plan:
+        parts = gather_group(jnp.concatenate(group) if len(group) > 1 else group[0], axis, sizes[axis])
+        start = 0
+        for s in group:
+            rows = s.shape[0]
+            out.append(absolute([p[start:start + rows] for p in parts], rows))
+            start += rows
+    return out
 
 
 def reduce_group(grads, axes, sizes):
@@ -259,8 +258,15 @@
     )
     values = matmul(normed_low, value_weight).astype(jnp.bfloat16)
     both = swap_halves(jnp.concatenate([keys, values], axis=1))
-    key_heads = both[:, :width].reshape(full_length, head_count, head_size)
-    value_heads = both[:, width:].reshape(full_length, head_count, head_size)
+    def heads(x, length):
+        return x.reshape(length, head_count, head_size).transpose(1, 0, 2)
+
+    def unheads(x):
+        return x.transpose(1, 0, 2).reshape(x.shape[1], width)
+
+    key_heads = heads(both[:, :width], full_length)
+    value_heads = heads(both[:, width:], full_length)
+    query_major = heads(query_heads.reshape(local_length, width), local_length)
     seg_local = lax.dynamic_slice_in_dim(seg_row, first_row, local_length)
     start_local = lax.dynamic_slice_in_dim(start_row, first_row, local_length)
     causal = columns[None, :] <= rows[:, None]
@@ -268,16 +274,18 @@
     allowed = (seg_local[:, None] == seg_row[None, :]) & (causal | same_piece)
 
     def scores_of(heads_in):
-        raw = jnp.einsum("qhd,khd->hqk", heads_in, key_heads, preferred_element_type=jnp.float32)
+        raw = jnp.einsum("hqd,hkd->hqk", heads_in, key_heads, preferred_element_type=jnp.float32)
         return jnp.where(allowed[None], raw * scale, -1e30)
 
-    scores = scores_of(query_heads)
+    scores = scores_of(query_major)
     highest = jnp.max(scores, axis=-1, keepdims=True)
     expd = jnp.exp(scores - highest)
     total = jnp.sum(expd, axis=-1, keepdims=True)
     log_total = highest + jnp.log(total)
-    probs_low = (expd / total).astype(jnp.bfloat16)
-    mixed = jnp.einsum("hqk,khd->qhd", probs_low, value_heads, preferred_element_type=jnp.float32)
+    probs_low = lax.optimization_barrier((expd / total).astype(jnp.bfloat16))
+    mixed = unheads(
+        jnp.einsum("hqk,hkd->hqd", probs_low, value_heads, preferred_element_type=jnp.float32)
+    )
     mixed_low = mixed.reshape(local_length, width).astype(jnp.bfloat16)
     after = hidden + matmul(mixed_low, out_weight)
     normed_two, norm_two_back = jax.vjp(layer_norm, after)
@@ -306,18 +314,22 @@
         .astype(jnp.bfloat16)
         .reshape(local_length, head_count, head_size)
     )
-    probs = jnp.exp(scores_of(query_heads) - log_total)
-    grad_probs = jnp.einsum("qhd,khd->hqk", grad_mixed, value_heads, preferred_element_type=jnp.float32)
+    mixed_major = heads(grad_mixed.reshape(local_length, width), local_length)
+    probs = jnp.exp(scores_of(query_major) - log_total)
+    grad_probs = jnp.einsum(
+        "hqd,hkd->hqk", mixed_major, value_heads, preferred_element_type=jnp.float32
+    )
     inner = jnp.sum(probs * grad_probs, axis=-1, keepdims=True)
-    grad_raw = (probs * (grad_probs - inner) * scale).astype(jnp.bfloat16)
-    grad_query = jnp.einsum("hqk,khd->qhd", grad_raw, key_heads, preferred_element_type=jnp.float32)
-    again_low = probs.astype(jnp.bfloat16)
-    grad_keys = jnp.einsum(
-        "hqk,qhd->khd", grad_raw, query_heads, preferred_element_type=jnp.float32
-    ).reshape(full_length, width)
-    grad_values = jnp.einsum(
-        "hqk,qhd->khd", again_low, grad_mixed, preferred_element_type=jnp.float32
-    ).reshape(full_length, width)
+    grad_raw = lax.optimization_barrier((probs * (grad_probs - inner) * scale).astype(jnp.bfloat16))
+    grad_query = unheads(
+        jnp.einsum("hqk,hkd->hqd", grad_raw, key_heads, preferred_element_type=jnp.float32)
+    ).reshape(local_length, head_count, head_size)
+    grad_keys = unheads(
+        jnp.einsum("hqk,hqd->hkd", grad_raw, query_major, preferred_element_type=jnp.float32)
+    )
+    grad_values = unheads(
+        jnp.einsum("hqk,hqd->hkd", probs_low, mixed_major, preferred_element_type=jnp.float32)
+    )
     grad_kv = jnp.concatenate([grad_keys, grad_values], axis=1)
     mine_kv = jnp.where(c == 0, grad_kv[:local_length], grad_kv[local_length:])
     theirs_kv = jnp.where(c == 0, grad_kv[local_length:], grad_kv[:local_length])
@@ -344,11 +356,14 @@
     grad_hidden = grad_after + norm_one_back(grad_normed)[0]
     input_grads = from_sequence(grad_hidden.astype(jnp.bfloat16))
 
-    wide = reduce_group([grads[4], grads[5]], (("y", 1, 2), ("z", 2, 1)), sizes)
-    narrow = reduce_group(
-        [grads[6], grads[3], grads[0], grads[1], grads[2]], (("y", 1, 2), ("z", 1, 2)), sizes
-    )
-    owned = [narrow[2], narrow[3], narrow[4], narrow[1], wide[0], wide[1], narrow[0]]
+    yz = (("y", 1, 2), ("z", 1, 2))
+    zy = (("z", 1, 2), ("y", 1, 2))
+    down = reduce_group([grads[6]], yz, sizes)
+    gate = reduce_group([grads[4]], zy, sizes)
+    up = reduce_group([grads[5]], yz, sizes)
+    out = reduce_group([grads[3]], zy, sizes)
+    qkv = reduce_group([grads[0], grads[1], grads[2]], yz, sizes)
+    owned = [qkv[0], qkv[1], qkv[2], out[0], gate[0], up[0], down[0]]
     return (output, input_grads, *owned)
 
 

time: 684 us -> 728 us (1.064)
  starting transfers between devices: 114 us -> 206 us
  matrix products: 215 us -> 133 us
  waiting for transfers between devices: 144 us -> 167 us
  other arithmetic: 93.5 us -> 110 us
    dot_general x6 -> x5, matrix products: 154 us -> 40.7 us  [the longest x1 12.1 us: scores_of(): jnp.einsum('hqd,hkd->hqk', heads_in, key_heads, preferred_element_type=jn...]
    ppermute x50 -> x125, starting transfers between devices: 83.7 us -> 163 us  [shift(): return lax.ppermute(x, axis, [(i, (i + step) % n) for i in range(n)])]
    sub x0 -> x1, matrix products: none -> 31.7 us  [body(): grad_probs - inner]
    unnamed x178 -> x189, local copies, waits for them, and re-layouts: 34.6 us -> 17.1 us
    ppermute x50 -> x125, waiting for transfers between devices: 125 us -> 140 us  [shift(): return lax.ppermute(x, axis, [(i, (i + step) % n) for i in range(n)])]
    dynamic_update_slice x39 -> x76, local copies, waits for them, and re-layouts: 32.6 us -> 46.6 us  [place(): return lax.dynamic_update_slice(buf, piece, start)]
    another operation x4 -> x10, other arithmetic: 19.4 us -> 10.5 us  [reduce_group(): pair = jnp.stack([own, oth])]
    convert_element_type x1, other arithmetic: 0.01 us -> 8.82 us  [body(): probs_low = lax.optimization_barrier((expd / total).astype(jnp.bfloat16))]
  transfers between devices with their start and end apart: 70 -> 160, of which waited for: 37 -> 59; matrix products, arithmetic and copies ran while one was open for 43% -> 30% of each run, Pallas kernels for 0% -> 0%
where the time goes in v1:
time: 728 us; the launch traced here: 717 us
  starting transfers between devices  206 us (28%)
  waiting for transfers between devices  167 us (23%)
  matrix products  133 us (18%)
  other arithmetic  110 us (15%)
  local copies, waits for them, and re-layouts  96.8 us (13%)
    ppermute x125, starting transfers between devices, shift(): return lax.ppermute(x, axis, [(i, (i + step) % n) for i in range(n)])  163 us
    ppermute x125, waiting for transfers between devices, shift(): return lax.ppermute(x, axis, [(i, (i + step) % n) for i in range(n)])  140 us
    dynamic_update_slice x76, local copies, waits for them, and re-layouts, place(): return lax.dynamic_update_slice(buf, piece, start)  46.6 us
    sub x1, matrix products, body(): grad_probs - inner  31.7 us
    dot_general x7, matrix products, matmul(): return jnp.dot(left, right, preferred_element_type=jnp.float32)  22.7 us
    ppermute x10, waiting for transfers between devices, cross(): return lax.ppermute(x, ('xl', 'xh'), [(i, 3 - i) for i in range(4)])  21.9 us
    dot_general x7, matrix products, contract_rows(): lax.dot_general(left, right, (((0,), (0,)), ((), ())), preferred_element_...  18.8 us
    dot_general x7, matrix products, contract_cols(): lax.dot_general(left, right, (((1,), (1,)), ((), ())), preferred_element_...  18.8 us
  transfers between devices with their start and end apart: 160, of which 59 were waited for; matrix products, arithmetic and copies ran while one was open for 30% of the time, Pallas kernels for 0%

profile of v1, /device:TPU:0, one launch (start us, length us, event | category | flops | bytes accessed | tf_op | source)
XLA Modules:
  0.0 716.9 jit_solution(18386692724303198113)
XLA Ops:
  45.8 11.4 %collective-permute-done.21 = bf16[48,3072]{1,0:T(8,128)(2,1)S(1)} collective-permute-done((bf16[48,3072]{1,0:T(8,128)(2,1)S(1)}, bf16[48,3072]{1,0:T(8,128)(2,1)S(1)}, u32[]{:S(2)}, u32[]{:S(2)}) %collective-permute-start.21) | collective-permute-done | bytes 294944 | tf_op jit(solution)/shard_map/ppermute | solution.py:108
  137.1 7.4 %fusion.176 = f32[512,3072]{1,0:T(8,128)} fusion(bf16[3072,768]{1,0:T(8,128)(2,1)S(1)} %slice_dynamic-update-slice_fusion, bf16[256,768]{1,0:T(8,128)(2,1)} %collective-permute-done.36, bf16[256,768]{1,0:T(8,128)(2,1)} %collective-permute-done.35, pred[]{:T(512)S(6)} %eq.180), kind=kOutput, calls=%fused_computation.539 | convolution fusion | flops 2419458048 | bytes 11796481 | tf_op jit(solution)/shard_map/dot_general | solution.py:43
  150.3 12.2 %maximum_select_fusion = bf16[1024,1536]{1,0:T(8,128)(2,1)S(1)} fusion(bf16[512,1536]{1,0:T(8,128)(2,1)S(1)} %collective-permute-done.8, bf16[512,768]{1,0:T(8,128)(2,1)S(1)} %convolution_convert_fusion.1, bf16[512,768]{1,0:T(8,128)(2,1)S(1)} %copy-done.24, pred[]{:T(512)S(6)} %eq.179), kind=kLoop, calls=%fused_computation.31 | loop fusion | flops 20447232 | bytes 6291457 | tf_op jit(solution)/shard_map/jit(_where)/select_n | solution.py:241
  166.2 12.1 %fusion.5 = (f32[12,512]{1,0:T(8,128)S(1)}, f32[12,512,1024]{2,1,0:T(8,128)}) fusion(pred[512,1024]{1,0:T(8,128)(4,1)S(1)} %fusion.27, bf16[12,1024,64]{1,2,0:T(8,128)(2,1)S(1)} %bitcast.171, bf16[512,12,32]{0,2,1:T(8,128)(2,1)} %get-tuple-element.60, bf16[512,12,32]{0,2,1:T(8,128)(2,1)S(1)} %copy-done.40), kind=kOutput, calls=%fused_computation.9 | convolution fusion | flops 825747456 | bytes 28073984 | tf_op jit(solution)/shard_map/hqd,hkd->hqk/dot_general | solution.py:277
  178.3 12.5 %fusion.2 = f32[12,512]{1,0:T(8,128)S(1)} fusion(f32[12,512,1024]{2,1,0:T(8,128)} %get-tuple-element.84, f32[12,512]{1,0:T(8,128)S(1)} %get-tuple-element.83, pred[512,1024]{1,0:T(8,128)(4,1)S(1)} %fusion.27), kind=kLoop, calls=%fused_computation.8 | loop fusion | flops 25159680 | bytes 25739264 | tf_op jit(solution)/shard_map/reduce_sum | solution.py:283
  193.7 8.8 %divide_convert_fusion = bf16[12,512,1024]{2,1,0:T(8,128)(2,1)} fusion(f32[12,512,1024]{2,1,0:T(8,128)S(1)} %copy-done, f32[12,512]{1,0:T(8,128)S(1)} %fusion.2, f32[12,512]{1,0:T(8,128)S(1)} %get-tuple-element.83, pred[512,1024]{1,0:T(8,128)(4,1)S(1)} %fusion.27), kind=kLoop, calls=%fused_computation.5 | loop fusion | flops 31457280 | bytes 38322176 | tf_op jit(solution)/shard_map/convert_element_type | solution.py:285
  204.7 9.0 %convolution_convert_fusion.2 = bf16[12,512,64]{1,2,0:T(8,128)(2,1)S(1)} fusion(bf16[12,512,1024]{2,1,0:T(8,128)(2,1)} %divide_convert_fusion, bf16[12,1024,64]{1,2,0:T(8,128)(2,1)} %bitcast.183), kind=kOutput, calls=%fused_computation.128 | convolution fusion | flops 805699584 | bytes 14942208 | tf_op jit(solution)/shard_map/hqk,hkd->hqd/dot_general | solution.py:287
  219.9 10.7 %add_convert_fusion = (bf16[512,3072]{1,0:T(8,128)(2,1)S(1)}, bf16[512,3072]{1,0:T(8,128)(2,1)S(1)}, bf16[512,3072]{1,0:T(8,128)(2,1)}) fusion(f32[512,3072]{1,0:T(8,128)} %fusion.176, f32[512,3072]{1,0:T(8,128)S(1)} %fusion.187, bf16[512,768]{1,0:T(8,128)(2,1)S(1)} %multiply_convert_fusion.3, bf16[768,3072]{1,0:T(8,128)(2,1)} %slice_dynamic-update-slice_fusion.4), kind=kOutput, calls=%fused_computation.17 | convolution fusion | flops 2444230656 | bytes 27525120 | tf_op jit(solution)/shard_map/dot_general | solution.py:33
  233.3 5.1 multiply_reduce_fusion.1
  244.2 5.0 fusion.194
  249.3 5.0 fusion.195
  257.9 4.9 collective-permute-start.33
  264.0 7.1 fusion.196
  271.1 31.7 %multiply_convert_fusion = bf16[12,512,1024]{2,1,0:T(8,128)(2,1)} fusion(f32[12,512,1024]{2,1,0:T(8,128)} %get-tuple-element.84, f32[12,512]{1,0:T(8,128)} %log_add_fusion, pred[512,1024]{1,0:T(8,128)(4,1)} %copy-done.19, bf16[12,512,64]{1,2,0:T(8,128)(2,1)} %bitcast.177, bf16[12,1024,64]{1,2,0:T(8,128)(2,1)} %bitcast.184), kind=kOutput, calls=%fused_computation.1 | convolution fusion | flops 1679825920 | bytes 40656896 | tf_op jit(solution)/shard_map/sub | solution.py:323
  302.8 10.1 %convolution_bitcast_fusion = f32[512,12,64]{0,2,1:T(8,128)} fusion(bf16[12,512,1024]{2,1,0:T(8,128)(2,1)} %multiply_convert_fusion, bf16[12,1024,64]{1,2,0:T(8,128)(2,1)} %bitcast.172), kind=kOutput, calls=%fused_computation.116 | convolution fusion | flops 805306368 | bytes 15728640 | tf_op jit(solution)/shard_map/hqk,hkd->hqd/dot_general | solution.py:325
  598.3 6.1 collective-permute-done.41
  604.5 5.9 collective-permute-done.47
  610.4 7.1 collective-permute-done.42
  617.6 5.9 collective-permute-done.48
  623.5 7.1 collective-permute-done.43
  630.7 5.9 collective-permute-done.49
  637.5 4.7 collective-permute-done.44
  646.4 5.4 collective-permute-done.45
  656.1 5.4 collective-permute-done.46
  (868 shorter events, 505.5 us)
Async XLA Ops:
  2.8 67.0 %collective-permute-start = (bf16[256,768]{1,0:T(8,128)(2,1)}, bf16[256,768]{1,0:T(8,128)(2,1)S(1)}, u32[]{:S(2)}, u32[]{:S(2)}) collective-permute-start(bf16[256,768]{1,0:T(8,128)(2,1)} %get-tuple-element.75), channel_id=1, source_target_pairs={{0,0},{1,2},{2,1},{3,3},{4,4},{5,6},{6,5},{7,7},{8,8},{9,10},{10,9... | collective-permute-start | bytes 1179656 | tf_op jit(solution)/shard_map/ppermute | solution.py:193
  4.6 65.3 %collective-permute-start.1 = (bf16[256,768]{1,0:T(8,128)(2,1)}, bf16[256,768]{1,0:T(8,128)(2,1)S(1)}, u32[]{:S(2)}, u32[]{:S(2)}) collective-permute-start(bf16[256,768]{1,0:T(8,128)(2,1)} %get-tuple-element.74), channel_id=1, source_target_pairs={{0,2},{1,0},{2,3},{3,1},{4,6},{5,4},{6,7},{7,5},{8,10},{9,8},{10,1... | collective-permute-start | bytes 1179656 | tf_op jit(solution)/shard_map/ppermute | solution.py:194
  10.6 32.4 %collective-permute-start.2 = (bf16[144,768]{1,0:T(8,128)(2,1)}, bf16[144,768]{1,0:T(8,128)(2,1)}, u32[]{:S(2)}, u32[]{:S(2)}) collective-permute-start(bf16[144,768]{1,0:T(8,128)(2,1)} %fusion.89), channel_id=1, source_target_pairs={{0,6},{2,4},{4,2},{6,0},{1,7},{3,5},{5,3},{7,1},{8,14},{10,12},{12... | collective-permute-start | bytes 663560 | tf_op jit(solution)/shard_map/ppermute | solution.py:108
  42.9 94.2 %collective-permute-start.36 = (bf16[256,768]{1,0:T(8,128)(2,1)}, bf16[256,768]{1,0:T(8,128)(2,1)}, u32[]{:S(2)}, u32[]{:S(2)}) collective-permute-start(bf16[256,768]{1,0:T(8,128)(2,1)} %get-tuple-element.71), channel_id=1, source_target_pairs={{0,2},{1,0},{2,3},{3,1},{4,6},{5,4},{6,7},{7,5},{8,10},{9,8},{10,1... | collective-permute-start | bytes 1179656 | tf_op jit(solution)/shard_map/ppermute | solution.py:194
  97.8 39.3 %collective-permute-start.35 = (bf16[256,768]{1,0:T(8,128)(2,1)}, bf16[256,768]{1,0:T(8,128)(2,1)}, u32[]{:S(2)}, u32[]{:S(2)}) collective-permute-start(bf16[256,768]{1,0:T(8,128)(2,1)} %get-tuple-element.70), channel_id=1, source_target_pairs={{0,0},{1,2},{2,1},{3,3},{4,4},{5,6},{6,5},{7,7},{8,8},{9,10},{10,9... | collective-permute-start | bytes 1179656 | tf_op jit(solution)/shard_map/ppermute | solution.py:193
  127.6 22.6 %collective-permute-start.8 = (bf16[512,1536]{1,0:T(8,128)(2,1)S(1)}, bf16[512,1536]{1,0:T(8,128)(2,1)S(1)}, u32[]{:S(2)}, u32[]{:S(2)}) collective-permute-start(bf16[512,1536]{1,0:T(8,128)(2,1)S(1)} %pad_maximum_fusion.8), channel_id=1, source_target_pairs={{0,1},{1,0},{2,3},{3,2},{4,5},{5,4},{6,7},{7,6},{8,9},{9,8},{10,11... | collective-permute-start | bytes 4718600 | tf_op jit(solution)/shard_map/ppermute | solution.py:240
  257.8 125.6 %collective-permute-start.34 = (bf16[256,768]{1,0:T(8,128)(2,1)}, bf16[256,768]{1,0:T(8,128)(2,1)S(1)}, u32[]{:S(2)}, u32[]{:S(2)}) collective-permute-start(bf16[256,768]{1,0:T(8,128)(2,1)} %get-tuple-element.73), channel_id=1, source_target_pairs={{2,0},{0,1},{3,2},{1,3},{6,4},{4,5},{7,6},{5,7},{10,8},{8,9},{11,1... | collective-permute-start | bytes 1179656 | tf_op jit(solution)/shard_map/ppermute | solution.py:205
  257.9 127.5 %collective-permute-start.33 = (bf16[256,768]{1,0:T(8,128)(2,1)}, bf16[256,768]{1,0:T(8,128)(2,1)}, u32[]{:S(2)}, u32[]{:S(2)}) collective-permute-start(bf16[256,768]{1,0:T(8,128)(2,1)} %get-tuple-element.72), channel_id=1, source_target_pairs={{0,0},{1,2},{2,1},{3,3},{4,4},{5,6},{6,5},{7,7},{8,8},{9,10},{10,9... | collective-permute-start | bytes 1179656 | tf_op jit(solution)/shard_map/ppermute | solution.py:204
  319.7 87.1 %collective-permute-start.88 = (bf16[384,3072]{1,0:T(8,128)(2,1)}, bf16[384,3072]{1,0:T(8,128)(2,1)}, u32[]{:S(2)}, u32[]{:S(2)}) collective-permute-start(bf16[384,3072]{1,0:T(8,128)(2,1)} %pad_maximum_fusion.4), channel_id=1, source_target_pairs={{0,1},{1,0},{2,3},{3,2},{4,5},{5,4},{6,7},{7,6},{8,9},{9,8},{10,11... | collective-permute-start | bytes 7077896 | tf_op jit(solution)/shard_map/ppermute | solution.py:112
  362.1 54.4 %collective-permute-start.112 = (bf16[384,3072]{1,0:T(8,128)(2,1)}, bf16[384,3072]{1,0:T(8,128)(2,1)}, u32[]{:S(2)}, u32[]{:S(2)}) collective-permute-start(bf16[384,3072]{1,0:T(8,128)(2,1)} %pad_maximum_fusion.5), channel_id=1, source_target_pairs={{0,1},{1,0},{2,3},{3,2},{4,5},{5,4},{6,7},{7,6},{8,9},{9,8},{10,11... | collective-permute-start | bytes 7077896 | tf_op jit(solution)/shard_map/ppermute | solution.py:112
  382.8 77.9 %collective-permute-start.37 = (f32[512,1536]{0,1:T(8,128)}, f32[512,1536]{0,1:T(8,128)}, u32[]{:S(2)}, u32[]{:S(2)}) collective-permute-start(f32[512,1536]{0,1:T(8,128)} %broadcast_select_fusion), channel_id=1, source_target_pairs={{0,1},{1,0},{2,3},{3,2},{4,5},{5,4},{6,7},{7,6},{8,9},{9,8},{10,11... | collective-permute-start | bytes 9437192 | tf_op jit(solution)/shard_map/ppermute | solution.py:336
  450.6 29.2 %collective-permute-start.91 = (bf16[2,48,1536]{2,1,0:T(8,128)(2,1)}, bf16[2,48,1536]{2,1,0:T(8,128)(2,1)}, u32[]{:S(2)}, u32[]{:S(2)}) collective-permute-start(bf16[2,48,1536]{2,1,0:T(8,128)(2,1)} %add_convert_fusion.11), channel_id=1, source_target_pairs={{0,8},{8,16},{16,24},{24,0},{1,9},{9,17},{17,25},{25,1},{2,10},{10... | collective-permute-start | bytes 884744 | tf_op jit(solution)/shard_map/ppermute | solution.py:49
  451.4 33.7 %collective-permute-start.97 = (bf16[2,48,1536]{2,1,0:T(8,128)(2,1)}, bf16[2,48,1536]{2,1,0:T(8,128)(2,1)}, u32[]{:S(2)}, u32[]{:S(2)}) collective-permute-start(bf16[2,48,1536]{2,1,0:T(8,128)(2,1)} %fusion.45), channel_id=1, source_target_pairs={{0,24},{8,0},{16,8},{24,16},{1,25},{9,1},{17,9},{25,17},{2,26},{10... | collective-permute-start | bytes 884744 | tf_op jit(solution)/shard_map/ppermute | solution.py:49
  455.9 30.4 %collective-permute-start.115 = (bf16[2,48,1536]{2,1,0:T(8,128)(2,1)}, bf16[2,48,1536]{2,1,0:T(8,128)(2,1)}, u32[]{:S(2)}, u32[]{:S(2)}) collective-permute-start(bf16[2,48,1536]{2,1,0:T(8,128)(2,1)} %add_convert_fusion.9), channel_id=1, source_target_pairs={{0,32},{32,64},{64,96},{96,0},{1,33},{33,65},{65,97},{97,1},{2,34}... | collective-permute-start | bytes 884744 | tf_op jit(solution)/shard_map/ppermute | solution.py:49
  456.7 31.7 %collective-permute-start.121 = (bf16[2,48,1536]{2,1,0:T(8,128)(2,1)}, bf16[2,48,1536]{2,1,0:T(8,128)(2,1)}, u32[]{:S(2)}, u32[]{:S(2)}) collective-permute-start(bf16[2,48,1536]{2,1,0:T(8,128)(2,1)} %fusion.55), channel_id=1, source_target_pairs={{0,96},{32,0},{64,32},{96,64},{1,97},{33,1},{65,33},{97,65},{2,98}... | collective-permute-start | bytes 884744 | tf_op jit(solution)/shard_map/ppermute | solution.py:49
  460.7 28.9 %collective-permute-start.139 = (bf16[2,192,384]{2,1,0:T(8,128)(2,1)}, bf16[2,192,384]{2,1,0:T(8,128)(2,1)}, u32[]{:S(2)}, u32[]{:S(2)}) collective-permute-start(bf16[2,192,384]{2,1,0:T(8,128)(2,1)} %add_convert_fusion.7), channel_id=1, source_target_pairs={{0,32},{32,64},{64,96},{96,0},{1,33},{33,65},{65,97},{97,1},{2,34}... | collective-permute-start | bytes 884744 | tf_op jit(solution)/shard_map/ppermute | solution.py:49
  485.2 44.3 %collective-permute-start.39 = (bf16[256,768]{1,0:T(8,128)(2,1)S(1)}, bf16[256,768]{1,0:T(8,128)(2,1)S(1)}, u32[]{:S(2)}, u32[]{:S(2)}) collective-permute-start(bf16[256,768]{1,0:T(8,128)(2,1)S(1)} %get-tuple-element.69), channel_id=1, source_target_pairs={{2,0},{0,1},{3,2},{1,3},{6,4},{4,5},{7,6},{5,7},{10,8},{8,9},{11,1... | collective-permute-start | bytes 1179656 | tf_op jit(solution)/shard_map/ppermute | solution.py:205
  486.3 43.2 %collective-permute-start.38 = (bf16[256,768]{1,0:T(8,128)(2,1)S(1)}, bf16[256,768]{1,0:T(8,128)(2,1)S(1)}, u32[]{:S(2)}, u32[]{:S(2)}) collective-permute-start(bf16[256,768]{1,0:T(8,128)(2,1)S(1)} %get-tuple-element.68), channel_id=1, source_target_pairs={{0,0},{1,2},{2,1},{3,3},{4,4},{5,6},{6,5},{7,7},{8,8},{9,10},{10,9... | collective-permute-start | bytes 1179656 | tf_op jit(solution)/shard_map/ppermute | solution.py:204
  555.7 37.7 %collective-permute-start.40 = (bf16[1152,768]{1,0:T(8,128)(2,1)}, bf16[1152,768]{1,0:T(8,128)(2,1)}, u32[]{:S(2)}, u32[]{:S(2)}) collective-permute-start(bf16[1152,768]{1,0:T(8,128)(2,1)} %copy-done.75), channel_id=1, source_target_pairs={{0,1},{1,0},{2,3},{3,2},{4,5},{5,4},{6,7},{7,6},{8,9},{9,8},{10,11... | collective-permute-start | bytes 5308424 | tf_op jit(solution)/shard_map/ppermute | solution.py:112
  579.9 85.9 %collective-permute-start.133 = (bf16[48,3072]{1,0:T(8,128)(2,1)}, bf16[48,3072]{1,0:T(8,128)(2,1)S(1)}, u32[]{:S(2)}, u32[]{:S(2)}) collective-permute-start(bf16[48,3072]{1,0:T(8,128)(2,1)} %dynamic_update_slice.377), channel_id=1, source_target_pairs={{0,96},{32,0},{64,32},{96,64},{1,97},{33,1},{65,33},{97,65},{2,98}... | collective-permute-start | bytes 884744 | tf_op jit(solution)/shard_map/ppermute | solution.py:49
  587.1 84.3 %collective-permute-start.156 = (bf16[192,768]{1,0:T(8,128)(2,1)}, bf16[192,768]{1,0:T(8,128)(2,1)S(1)}, u32[]{:S(2)}, u32[]{:S(2)}) collective-permute-start(bf16[192,768]{1,0:T(8,128)(2,1)} %maximum_dynamic-update-slice_fusion.10), channel_id=1, source_target_pairs={{0,32},{32,64},{64,96},{96,0},{1,33},{33,65},{65,97},{97,1},{2,34}... | collective-permute-start | bytes 884744 | tf_op jit(solution)/shard_map/ppermute | solution.py:49
  588.1 89.3 %collective-permute-start.157 = (bf16[192,768]{1,0:T(8,128)(2,1)}, bf16[192,768]{1,0:T(8,128)(2,1)S(1)}, u32[]{:S(2)}, u32[]{:S(2)}) collective-permute-start(bf16[192,768]{1,0:T(8,128)(2,1)} %maximum_dynamic-update-slice_fusion.10), channel_id=1, source_target_pairs={{0,96},{32,0},{64,32},{96,64},{1,97},{33,1},{65,33},{97,65},{2,98}... | collective-permute-start | bytes 884744 | tf_op jit(solution)/shard_map/ppermute | solution.py:49
  593.4 90.5 %collective-permute-start.111 = (bf16[24,3072]{1,0:T(8,128)(2,1)S(1)}, bf16[24,3072]{1,0:T(8,128)(2,1)S(1)}, u32[]{:S(2)}, u32[]{:S(2)}) collective-permute-start(bf16[24,3072]{1,0:T(8,128)(2,1)S(1)} %slice.540), channel_id=1, source_target_pairs={{0,24},{8,0},{16,8},{24,16},{1,25},{9,1},{17,9},{25,17},{2,26},{10... | collective-permute-start | bytes 442376 | tf_op jit(solution)/shard_map/ppermute | solution.py:49
  670.2 22.7 %collective-permute-start.135 = (bf16[24,3072]{1,0:T(8,128)(2,1)S(1)}, bf16[24,3072]{1,0:T(8,128)(2,1)S(1)}, u32[]{:S(2)}, u32[]{:S(2)}) collective-permute-start(bf16[24,3072]{1,0:T(8,128)(2,1)S(1)} %slice.552), channel_id=1, source_target_pairs={{0,96},{32,0},{64,32},{96,64},{1,97},{33,1},{65,33},{97,65},{2,98}... | collective-permute-start | bytes 442376 | tf_op jit(solution)/shard_map/ppermute | solution.py:49
  (228 other events, 2370.3 us)

commit v2 on v1

--- a/solution.py
+++ b/solution.py
@@ -55,15 +55,17 @@
     return lax.dynamic_update_slice(buf, piece, start)
 
 
-def ring_gather(piece, axis, n, dim):
+def ring_gather(piece, axis, n, dim, direct=False):
     if n == 1:
         return piece
     me = lax.axis_index(axis)
     shape = list(piece.shape)
     shape[dim] *= n
     buf = place(jnp.zeros(shape, piece.dtype), piece, me, dim)
-    if n == 2:
-        return place(buf, shift(piece, axis, 2, 1), 1 - me, dim)
+    if n == 2 or direct:
+        for k in range(1, n):
+            buf = place(buf, shift(piece, axis, n, k), (me - k) % n, dim)
+        return buf
     back = piece
     ahead = piece
     for step in range(1, n // 2 + 1):
@@ -80,28 +82,39 @@
     return buf
 
 
-def ring_reduce(x, axis, n, dim, hdim):
+def ring_reduce(x, axis, n, dim, hdim, direct=False):
     if n == 1:
         return x
     me = lax.axis_index(axis)
     size = x.shape[dim] // n
 
-    def chunk(k, part):
-        return lax.dynamic_slice_in_dim(part, k * size, size, axis=dim)
-
-    if n == 2:
-        sent = shift(chunk(1 - me, x).astype(jnp.bfloat16), axis, 2, 1)
-        return chunk(me, x) + sent.astype(jnp.float32)
+    def chunk(k):
+        return lax.dynamic_slice_in_dim(x, (k % n) * size, size, axis=dim)
+
+    def low(v):
+        return v.astype(jnp.bfloat16)
+
+    if n == 2 or direct:
+        acc = chunk(me)
+        for k in range(1, n):
+            acc = acc + shift(low(chunk(me + k)), axis, n, k).astype(jnp.float32)
+        return acc
+    assert n == 4
     half = x.shape[hdim] // 2
-    parts = []
-    for direction, lo, hi in ((1, 0, half), (-1, half, x.shape[hdim])):
-        part = lax.slice_in_dim(x, lo, hi, axis=hdim)
-        acc = chunk((me - direction) % n, part)
-        for step in range(n - 1):
-            got = shift(acc.astype(jnp.bfloat16), axis, n, direction)
-            acc = got.astype(jnp.float32) + chunk((me - direction * (step + 2)) % n, part)
-        parts.append(acc)
-    return jnp.concatenate(parts, axis=hdim)
+
+    def part(k, which):
+        c = chunk(k)
+        return lax.slice_in_dim(c, 0, half, axis=hdim) if which == 0 else lax.slice_in_dim(
+            c, half, c.shape[hdim], axis=hdim
+        )
+
+    from_ahead = shift(low(jnp.stack([part(me - 2, 0), part(me - 1, 1)])), axis, n, -1)
+    from_back = shift(low(jnp.stack([part(me + 2, 1), part(me + 1, 0)])), axis, n, 1)
+    relay_ahead = shift(low(from_ahead[0].astype(jnp.float32) + part(me - 1, 0)), axis, n, -1)
+    relay_back = shift(low(from_back[0].astype(jnp.float32) + part(me + 1, 1)), axis, n, 1)
+    first = part(me, 0) + from_back[1].astype(jnp.float32) + relay_ahead.astype(jnp.float32)
+    second = part(me, 1) + from_ahead[1].astype(jnp.float32) + relay_back.astype(jnp.float32)
+    return jnp.concatenate([first, second], axis=hdim)
 
 
 def cross(x):
@@ -120,11 +133,11 @@
     return buf
 
 
-def gather_group(own, axis, n):
+def gather_group(own, axis, n, direct):
     size = own.shape[0] // n
     me = lax.axis_index(axis)
     mine = lax.dynamic_slice_in_dim(own, me * size, size, axis=0)
-    other = ring_gather(cross(mine), axis, n, 0)
+    other = ring_gather(cross(mine), axis, n, 0, direct)
     partner = swap_core(jnp.concatenate([own, other]))
     rows = own.shape[0]
     return [own, partner[:rows], other, partner[rows:]]
@@ -133,26 +146,23 @@
 def gather_weights(shards, sizes):
     w_query, w_key, w_value, w_out, w_gate, w_up, w_down = shards
     plan = (
-        ((w_query, w_key, w_value), "y"),
-        ((w_out,), "z"),
-        ((w_gate,), "y"),
-        ((w_up,), "z"),
-        ((w_down,), "z"),
-    )
-    out = []
-    for group, axis in plan:
-        parts = gather_group(jnp.concatenate(group) if len(group) > 1 else group[0], axis, sizes[axis])
+        ((w_query, w_key, w_value), "y", True),
+        ((w_out, w_down), "z", False),
+        ((w_gate, w_up), "y", False),
+    )
+    out = {}
+    for group, axis, direct in plan:
+        parts = gather_group(jnp.concatenate(group), axis, sizes[axis], direct)
         start = 0
         for s in group:
             rows = s.shape[0]
-            out.append(absolute([p[start:start + rows] for p in parts], rows))
+            out[id(s)] = absolute([p[start:start + rows] for p in parts], rows)
             start += rows
-    return out
-
-
-def reduce_group(grads, axes, sizes):
+    return [out[id(s)] for s in shards]
+
+
+def reduce_group(grads, sizes, direct):
     g = lax.axis_index("xh") * 2 + lax.axis_index("c")
-    xl = lax.axis_index("xl")
 
     def shard(w, j):
         rows = w.shape[0] // 4
@@ -164,20 +174,17 @@
     own = jnp.concatenate([shard(w, 0) for w in grads]) + got[:total]
     oth = jnp.concatenate([shard(w, 2) for w in grads]) + got[total:]
     pair = jnp.stack([own, oth])
-    for axis, dim, hdim in axes:
-        pair = ring_reduce(pair, axis, sizes[axis], dim, hdim)
-    size = pair.shape[2] // 2
-    own_keep = lax.dynamic_slice_in_dim(pair[0], xl * size, size, axis=1)
-    own_send = lax.dynamic_slice_in_dim(pair[0], (1 - xl) * size, size, axis=1)
-    oth_keep = lax.dynamic_slice_in_dim(pair[1], (1 - xl) * size, size, axis=1)
-    oth_send = lax.dynamic_slice_in_dim(pair[1], xl * size, size, axis=1)
-    got = lax.ppermute(
-        jnp.stack([own_send, oth_send]).astype(jnp.bfloat16), "xl", [(0, 1), (1, 0)]
-    ).astype(jnp.float32)
-    mine = own_keep + got[0] + cross((oth_keep + got[1]).astype(jnp.bfloat16)).astype(jnp.float32)
-    full = ring_gather(mine.astype(jnp.bfloat16), "xl", 2, 1)
-    for axis, dim, _ in reversed(axes):
-        full = ring_gather(full, axis, sizes[axis], dim - 1)
+    pair = ring_reduce(pair, "y", sizes["y"], 1, 2, direct)
+    pair = ring_reduce(pair, "z", sizes["z"], 1, 2, direct)
+    low = pair.astype(jnp.bfloat16)
+    mine = (
+        pair[0]
+        + lax.ppermute(low[0], "xl", [(0, 1), (1, 0)]).astype(jnp.float32)
+        + cross(low[1]).astype(jnp.float32)
+        + lax.ppermute(low[1], "xh", [(0, 1), (1, 0)]).astype(jnp.float32)
+    )
+    full = ring_gather(mine.astype(jnp.bfloat16), "z", sizes["z"], 0, direct)
+    full = ring_gather(full, "y", sizes["y"], 0, direct)
     out = []
     start = 0
     for w in grads:
@@ -356,14 +363,15 @@
     grad_hidden = grad_after + norm_one_back(grad_normed)[0]
     input_grads = from_sequence(grad_hidden.astype(jnp.bfloat16))
 
-    yz = (("y", 1, 2), ("z", 1, 2))
-    zy = (("z", 1, 2), ("y", 1, 2))
-    down = reduce_group([grads[6]], yz, sizes)
-    gate = reduce_group([grads[4]], zy, sizes)
-    up = reduce_group([grads[5]], yz, sizes)
-    out = reduce_group([grads[3]], zy, sizes)
-    qkv = reduce_group([grads[0], grads[1], grads[2]], yz, sizes)
-    owned = [qkv[0], qkv[1], qkv[2], out[0], gate[0], up[0], down[0]]
+    width = grads[6].shape[1]
+    gate_rows = grads[4].shape[0]
+    early = reduce_group(
+        [grads[6], grads[4].reshape(-1, width), grads[5].reshape(-1, width), grads[3]], sizes, False
+    )
+    late = reduce_group([grads[0], grads[1], grads[2]], sizes, True)
+    gate_grad = early[1].reshape(gate_rows // 4, -1)
+    up_grad = early[2].reshape(gate_rows // 4, -1)
+    owned = [late[0], late[1], late[2], early[3], gate_grad, up_grad, early[0]]
     return (output, input_grads, *owned)
 
 

time: 728 us -> 669 us (0.919)
  starting transfers between devices: 206 us -> 94 us
  local copies, waits for them, and re-layouts: 96.8 us -> 143 us
  matrix products: 133 us -> 147 us
  waiting for transfers between devices: 167 us -> 159 us
    ppermute x125 -> x39, starting transfers between devices: 163 us -> 60.4 us  [shift(): return lax.ppermute(x, axis, [(i, (i + step) % n) for i in range(n)])]
    reshape x0 -> x4, local copies, waits for them, and re-layouts: none -> 28.2 us  [the longest x1 11.5 us: body(): grads[5].reshape(-1, width)]
    unnamed x189 -> x204, local copies, waits for them, and re-layouts: 17.1 us -> 36.3 us
    ppermute x10 -> x5, waiting for transfers between devices: 21.9 us -> 3.18 us  [cross(): return lax.ppermute(x, ('xl', 'xh'), [(i, 3 - i) for i in range(4)])]
    dynamic_slice x3 -> x7, local copies, waits for them, and re-layouts: 1.27 us -> 14.2 us  [shard(): lax.dynamic_slice_in_dim(w, jnp.bitwise_xor(g, j) * rows, rows, axis=0)]
    another operation x10 -> x3, other arithmetic: 10.5 us -> 23 us  [reduce_group(): pair = jnp.stack([own, oth])]
    dynamic_update_slice x76 -> x47, local copies, waits for them, and re-layouts: 46.6 us -> 36.1 us  [place(): return lax.dynamic_update_slice(buf, piece, start)]
    ppermute x125 -> x39, waiting for transfers between devices: 140 us -> 150 us  [shift(): return lax.ppermute(x, axis, [(i, (i + step) % n) for i in range(n)])]
  transfers between devices with their start and end apart: 160 -> 63, of which waited for: 59 -> 27; matrix products, arithmetic and copies ran while one was open for 30% -> 37% of each run, Pallas kernels for 0% -> 0%
where the time goes in v2:
time: 669 us; the launch traced here: 657 us
  waiting for transfers between devices  159 us (24%)
  matrix products  147 us (22%)
  local copies, waits for them, and re-layouts  143 us (21%)
  other arithmetic  112 us (17%)
  starting transfers between devices  94 us (14%)
    ppermute x39, waiting for transfers between devices, shift(): return lax.ppermute(x, axis, [(i, (i + step) % n) for i in range(n)])  150 us
    ppermute x39, starting transfers between devices, shift(): return lax.ppermute(x, axis, [(i, (i + step) % n) for i in range(n)])  60.4 us
    unnamed x204, local copies, waits for them, and re-layouts  36.3 us
    dynamic_update_slice x47, local copies, waits for them, and re-layouts, place(): return lax.dynamic_update_slice(buf, piece, start)  36.1 us
    sub x1, matrix products, body(): grad_probs - inner  32.9 us
    dot_general x7, matrix products, matmul(): return jnp.dot(left, right, preferred_element_type=jnp.float32)  27.5 us
    dot_general x7, matrix products, contract_cols(): lax.dot_general(left, right, (((1,), (1,)), ((), ())), preferred_element_...  24.3 us
    another operation x3, other arithmetic, reduce_group(): pair = jnp.stack([own, oth])  23 us
  transfers between devices with their start and end apart: 63, of which 27 were waited for; matrix products, arithmetic and copies ran while one was open for 37% of the time, Pallas kernels for 0%

profile of v2, /device:TPU:0, one launch (start us, length us, event | category | flops | bytes accessed | tf_op | source)
XLA Modules:
  0.0 657.4 jit_solution(5546952744353105222)
XLA Ops:
  46.3 7.3 %collective-permute-done.10 = bf16[240,768]{1,0:T(8,128)(2,1)S(1)} collective-permute-done((bf16[240,768]{1,0:T(8,128)(2,1)}, bf16[240,768]{1,0:T(8,128)(2,1)S(1)}, u32[]{:S(2)}, u32[]{:S(2)}) %collective-permute-start.10) | collective-permute-done | bytes 368672 | tf_op jit(solution)/shard_map/ppermute | solution.py:49
  77.5 12.4 %collective-permute-done.16 = bf16[96,3072]{1,0:T(8,128)(2,1)S(1)} collective-permute-done((bf16[96,3072]{1,0:T(8,128)(2,1)S(1)}, bf16[96,3072]{1,0:T(8,128)(2,1)S(1)}, u32[]{:S(2)}, u32[]{:S(2)}) %collective-permute-start.16) | collective-permute-done | bytes 589856 | tf_op jit(solution)/shard_map/ppermute | solution.py:49
  126.8 8.2 %fusion.110 = f32[512,3072]{1,0:T(8,128)} fusion(bf16[3072,768]{1,0:T(8,128)(2,1)} %slice_dynamic-update-slice_fusion, bf16[256,768]{1,0:T(8,128)(2,1)} %collective-permute-done.23, bf16[256,768]{1,0:T(8,128)(2,1)} %collective-permute-done.22, pred[]{:T(512)S(6)} %eq.100), kind=kOutput, calls=%fused_computation.345 | convolution fusion | flops 2419458048 | bytes 11796481 | tf_op jit(solution)/shard_map/dot_general | solution.py:43
  135.0 12.6 %maximum_select_fusion = bf16[1024,1536]{1,0:T(8,128)(2,1)S(1)} fusion(bf16[512,1536]{1,0:T(8,128)(2,1)S(1)} %collective-permute-done.7, bf16[512,768]{1,0:T(8,128)(2,1)S(1)} %copy-done.39, bf16[512,768]{1,0:T(8,128)(2,1)S(1)} %copy-done.31, pred[]{:T(512)S(6)} %eq.99), kind=kLoop, calls=%fused_computation.59 | loop fusion | flops 20447232 | bytes 6291457 | tf_op jit(solution)/shard_map/jit(_where)/select_n | solution.py:248
  152.1 14.4 %fusion.5 = (f32[12,512]{1,0:T(8,128)S(1)}, f32[12,512,1024]{2,1,0:T(8,128)}) fusion(pred[512,1024]{1,0:T(8,128)(4,1)} %fusion.23, bf16[12,1024,64]{1,2,0:T(8,128)(2,1)} %bitcast.200, bf16[512,12,32]{0,2,1:T(8,128)(2,1)} %get-tuple-element.66, bf16[512,12,32]{0,2,1:T(8,128)(2,1)S(1)} %get-tuple-element.65), kind=kOutput, calls=%fused_computation.19 | convolution fusion | flops 825747456 | bytes 28073984 | tf_op jit(solution)/shard_map/hqd,hkd->hqk/dot_general | solution.py:284
  166.5 12.6 %fusion.2 = f32[12,512]{1,0:T(8,128)S(1)} fusion(f32[12,512,1024]{2,1,0:T(8,128)} %get-tuple-element.99, f32[12,512]{1,0:T(8,128)S(1)} %get-tuple-element.98, pred[512,1024]{1,0:T(8,128)(4,1)S(1)} %copy-done.21), kind=kLoop, calls=%fused_computation.18 | loop fusion | flops 25159680 | bytes 25739264 | tf_op jit(solution)/shard_map/reduce_sum | solution.py:290
  181.9 8.9 %divide_convert_fusion = bf16[12,512,1024]{2,1,0:T(8,128)(2,1)} fusion(f32[12,512,1024]{2,1,0:T(8,128)S(1)} %copy-done, f32[12,512]{1,0:T(8,128)S(1)} %fusion.2, f32[12,512]{1,0:T(8,128)S(1)} %get-tuple-element.98, pred[512,1024]{1,0:T(8,128)(4,1)S(1)} %copy-done.21), kind=kLoop, calls=%fused_computation.15 | loop fusion | flops 31457280 | bytes 38322176 | tf_op jit(solution)/shard_map/convert_element_type | solution.py:292
  193.3 9.8 %convolution_convert_fusion.2 = bf16[12,512,64]{1,2,0:T(8,128)(2,1)} fusion(bf16[12,512,1024]{2,1,0:T(8,128)(2,1)} %divide_convert_fusion, bf16[12,1024,64]{1,2,0:T(8,128)(2,1)} %bitcast.212), kind=kOutput, calls=%fused_computation.123 | convolution fusion | flops 805699584 | bytes 14942208 | tf_op jit(solution)/shard_map/hqk,hkd->hqd/dot_general | solution.py:294
  221.3 9.0 %add_convert_fusion = (bf16[512,3072]{1,0:T(8,128)(2,1)S(1)}, bf16[512,3072]{1,0:T(8,128)(2,1)S(1)}, bf16[512,3072]{1,0:T(8,128)(2,1)}) fusion(f32[512,3072]{1,0:T(8,128)S(1)} %bitcast.224, f32[512,3072]{1,0:T(8,128)S(1)} %fusion.117, bf16[512,768]{1,0:T(8,128)(2,1)S(1)} %multiply_convert_fusion.3, bf16[768,3072]{1,0:T(8,128)(2,1)} %get-tuple-element.29), kind=kOutput, calls=%fused_computation.41 | convolution fusion | flops 2444230656 | bytes 27525120 | tf_op jit(solution)/shard_map/dot_general | solution.py:33
  258.8 32.9 %multiply_convert_fusion = bf16[12,512,1024]{2,1,0:T(8,128)(2,1)} fusion(f32[12,512,1024]{2,1,0:T(8,128)} %get-tuple-element.99, f32[12,512]{1,0:T(8,128)S(1)} %log_add_fusion, pred[512,1024]{1,0:T(8,128)(4,1)S(1)} %copy-done.22, bf16[12,512,64]{1,2,0:T(8,128)(2,1)} %bitcast.205, bf16[12,1024,64]{1,2,0:T(8,128)(2,1)} %bitcast.213), kind=kOutput, calls=%fused_computation.11 | convolution fusion | flops 1679825920 | bytes 40656896 | tf_op jit(solution)/shard_map/sub | solution.py:330
  301.5 11.5 %reshape.318 = f32[3072,768]{1,0:T(8,128)} reshape(f32[768,3072]{1,0:T(8,128)} %fusion.123) | data formatting | bytes 18874368 | tf_op jit(solution)/shard_map/reshape | solution.py:369
  313.0 11.5 %reshape.319 = f32[3072,768]{1,0:T(8,128)} reshape(f32[768,3072]{1,0:T(8,128)} %fusion.124) | data formatting | bytes 18874368 | tf_op jit(solution)/shard_map/reshape | solution.py:369
  340.6 7.1 %fusion.63 = f32[12,1024,64]{1,2,0:T(8,128)S(1)} fusion(bf16[12,512,1024]{2,1,0:T(8,128)(2,1)} %multiply_convert_fusion, bf16[512,12,32]{0,2,1:T(8,128)(2,1)S(1)} %copy-done.38, bf16[512,12,32]{0,2,1:T(8,128)(2,1)S(1)} %copy-done.37), kind=kOutput, calls=%fused_computation.198 | convolution fusion | flops 806879232 | bytes 16515072 | tf_op jit(solution)/shard_map/hqk,hqd->hkd/dot_general | solution.py:335
  353.4 6.5 add_convert_fusion.2
  379.5 10.1 %convolution_bitcast_fusion = f32[512,12,64]{0,2,1:T(8,128)} fusion(bf16[12,512,1024]{2,1,0:T(8,128)(2,1)} %multiply_convert_fusion, bf16[12,1024,64]{1,2,0:T(8,128)(2,1)} %bitcast.201), kind=kOutput, calls=%fused_computation.117 | convolution fusion | flops 805306368 | bytes 15728640 | tf_op jit(solution)/shard_map/hqk,hkd->hqd/dot_general | solution.py:332
  402.0 9.9 %convert_element_type.289 = f32[4992,768]{1,0:T(8,128)} convert(bf16[4992,768]{1,0:T(8,128)(2,1)} %collective-permute-done.43) | non-fusion elementwise | flops 3833856 | bytes 23003136 | tf_op jit(solution)/shard_map/convert_element_type | solution.py:172
  412.0 16.3 %fusion.10 = (f32[1,2496,768]{2,1,0:T(8,128)}, f32[1,2496,768]{2,1,0:T(8,128)}) fusion(f32[4992,768]{1,0:T(8,128)} %convert_element_type.289, f32[192,768]{1,0:T(8,128)} %get-tuple-element.48, f32[768,768]{1,0:T(8,128)S(1)} %copy-done.20, f32[768,768]{1,0:T(8,128)} %get-tuple-element.25, f32[768,768]{1,0:T(8,128)} %get-tuple-element.23, ...), kind=kLoop, calls=%fused_computation.25 | loop fusion | flops 15335424 | bytes 46006272 | tf_op jit(solution)/shard_map/stack | solution.py:176
  428.3 6.2 fusion.14
  450.5 35.5 %collective-permute-done.44 = bf16[2,2,624,384]{3,2,1,0:T(8,128)(2,1)S(1)} collective-permute-done((bf16[2,2,624,384]{3,2,1,0:T(8,128)(2,1)S(1)}, bf16[2,2,624,384]{3,2,1,0:T(8,128)(2,1)S(1)}, u32[]{:S(2)}, u32[]{:S(2)}) %collective-permute-start.44) | collective-permute-done | bytes 1916960 | tf_op jit(solution)/shard_map/ppermute | solution.py:49
  494.9 16.0 %collective-permute-done.47 = bf16[2,624,384]{2,1,0:T(8,128)(2,1)S(1)} collective-permute-done((bf16[2,624,384]{2,1,0:T(8,128)(2,1)S(1)}, bf16[2,624,384]{2,1,0:T(8,128)(2,1)S(1)}, u32[]{:S(2)}, u32[]{:S(2)}) %collective-permute-start.47) | collective-permute-done | bytes 958496 | tf_op jit(solution)/shard_map/ppermute | solution.py:49
  517.0 9.0 %collective-permute-done.48 = bf16[2,2,156,384]{3,2,1,0:T(8,128)(2,1)S(1)} collective-permute-done((bf16[2,2,156,384]{3,2,1,0:T(8,128)(2,1)S(1)}, bf16[2,2,156,384]{3,2,1,0:T(8,128)(2,1)S(1)}, u32[]{:S(2)}, u32[]{:S(2)}) %collective-permute-start.48) | collective-permute-done | bytes 479264 | tf_op jit(solution)/shard_map/ppermute | solution.py:49
  538.5 12.2 %collective-permute-done.30 = bf16[2,144,768]{2,1,0:T(8,128)(2,1)S(1)} collective-permute-done((bf16[2,144,768]{2,1,0:T(8,128)(2,1)S(1)}, bf16[2,144,768]{2,1,0:T(8,128)(2,1)S(1)}, u32[]{:S(2)}, u32[]{:S(2)}) %collective-permute-start.30) | collective-permute-done | bytes 442400 | tf_op jit(solution)/shard_map/ppermute | solution.py:49
  596.2 6.2 collective-permute-done.37
  637.0 7.9 %collective-permute-done.62 = bf16[312,768]{1,0:T(8,128)(2,1)S(1)} collective-permute-done((bf16[312,768]{1,0:T(8,128)(2,1)S(1)}, bf16[312,768]{1,0:T(8,128)(2,1)S(1)}, u32[]{:S(2)}, u32[]{:S(2)}) %collective-permute-start.62) | collective-permute-done | bytes 479264 | tf_op jit(solution)/shard_map/ppermute | solution.py:49
  (512 shorter events, 360.6 us)
Async XLA Ops:
  2.9 39.1 %collective-permute-start = (bf16[256,768]{1,0:T(8,128)(2,1)}, bf16[256,768]{1,0:T(8,128)(2,1)S(1)}, u32[]{:S(2)}, u32[]{:S(2)}) collective-permute-start(bf16[256,768]{1,0:T(8,128)(2,1)} %get-tuple-element.86), channel_id=1, source_target_pairs={{0,0},{1,2},{2,1},{3,3},{4,4},{5,6},{6,5},{7,7},{8,8},{9,10},{10,9... | collective-permute-start | bytes 1179656 | tf_op jit(solution)/shard_map/ppermute | solution.py:200
  4.5 38.9 %collective-permute-start.1 = (bf16[256,768]{1,0:T(8,128)(2,1)}, bf16[256,768]{1,0:T(8,128)(2,1)S(1)}, u32[]{:S(2)}, u32[]{:S(2)}) collective-permute-start(bf16[256,768]{1,0:T(8,128)(2,1)} %get-tuple-element.85), channel_id=1, source_target_pairs={{0,2},{1,0},{2,3},{3,1},{4,6},{5,4},{6,7},{7,5},{8,10},{9,8},{10,1... | collective-permute-start | bytes 1179656 | tf_op jit(solution)/shard_map/ppermute | solution.py:201
  9.9 29.3 %collective-permute-start.8 = (bf16[240,768]{1,0:T(8,128)(2,1)}, bf16[240,768]{1,0:T(8,128)(2,1)}, u32[]{:S(2)}, u32[]{:S(2)}) collective-permute-start(bf16[240,768]{1,0:T(8,128)(2,1)} %fusion.79), channel_id=1, source_target_pairs={{0,6},{2,4},{4,2},{6,0},{1,7},{3,5},{5,3},{7,1},{8,14},{10,12},{12... | collective-permute-start | bytes 1105928 | tf_op jit(solution)/shard_map/ppermute | solution.py:121
  11.5 23.5 %collective-permute-start.2 = (bf16[144,768]{1,0:T(8,128)(2,1)}, bf16[144,768]{1,0:T(8,128)(2,1)}, u32[]{:S(2)}, u32[]{:S(2)}) collective-permute-start(bf16[144,768]{1,0:T(8,128)(2,1)} %fusion.95), channel_id=1, source_target_pairs={{0,6},{2,4},{4,2},{6,0},{1,7},{3,5},{5,3},{7,1},{8,14},{10,12},{12... | collective-permute-start | bytes 663560 | tf_op jit(solution)/shard_map/ppermute | solution.py:121
  16.2 110.6 %collective-permute-start.23 = (bf16[256,768]{1,0:T(8,128)(2,1)}, bf16[256,768]{1,0:T(8,128)(2,1)}, u32[]{:S(2)}, u32[]{:S(2)}) collective-permute-start(bf16[256,768]{1,0:T(8,128)(2,1)} %get-tuple-element.82), channel_id=1, source_target_pairs={{0,2},{1,0},{2,3},{3,1},{4,6},{5,4},{6,7},{7,5},{8,10},{9,8},{10,1... | collective-permute-start | bytes 1179656 | tf_op jit(solution)/shard_map/ppermute | solution.py:201
  35.9 37.7 %collective-permute-start.14 = (bf16[96,3072]{1,0:T(8,128)(2,1)S(1)}, bf16[96,3072]{1,0:T(8,128)(2,1)S(1)}, u32[]{:S(2)}, u32[]{:S(2)}) collective-permute-start(bf16[96,3072]{1,0:T(8,128)(2,1)S(1)} %copy-done.64), channel_id=1, source_target_pairs={{0,6},{2,4},{4,2},{6,0},{1,7},{3,5},{5,3},{7,1},{8,14},{10,12},{12... | collective-permute-start | bytes 1769480 | tf_op jit(solution)/shard_map/ppermute | solution.py:121
  39.2 26.3 %collective-permute-start.3 = (bf16[144,768]{1,0:T(8,128)(2,1)}, bf16[144,768]{1,0:T(8,128)(2,1)S(1)}, u32[]{:S(2)}, u32[]{:S(2)}) collective-permute-start(bf16[144,768]{1,0:T(8,128)(2,1)} %collective-permute-done.2), channel_id=1, source_target_pairs={{0,32},{32,64},{64,96},{96,0},{1,33},{33,65},{65,97},{97,1},{2,34}... | collective-permute-start | bytes 663560 | tf_op jit(solution)/shard_map/ppermute | solution.py:49
  65.2 40.0 %collective-permute-start.13 = (bf16[1920,768]{1,0:T(8,128)(2,1)S(1)}, bf16[1920,768]{1,0:T(8,128)(2,1)S(1)}, u32[]{:S(2)}, u32[]{:S(2)}) collective-permute-start(bf16[1920,768]{1,0:T(8,128)(2,1)S(1)} %pad_maximum_fusion.2), channel_id=1, source_target_pairs={{0,1},{1,0},{2,3},{3,2},{4,5},{5,4},{6,7},{7,6},{8,9},{9,8},{10,11... | collective-permute-start | bytes 8847368 | tf_op jit(solution)/shard_map/ppermute | solution.py:125
  77.1 28.1 %collective-permute-start.6 = (bf16[1152,768]{1,0:T(8,128)(2,1)S(1)}, bf16[1152,768]{1,0:T(8,128)(2,1)S(1)}, u32[]{:S(2)}, u32[]{:S(2)}) collective-permute-start(bf16[1152,768]{1,0:T(8,128)(2,1)S(1)} %pad_maximum_fusion.5), channel_id=1, source_target_pairs={{0,1},{1,0},{2,3},{3,2},{4,5},{5,4},{6,7},{7,6},{8,9},{9,8},{10,11... | collective-permute-start | bytes 5308424 | tf_op jit(solution)/shard_map/ppermute | solution.py:125
  98.3 28.5 %collective-permute-start.22 = (bf16[256,768]{1,0:T(8,128)(2,1)}, bf16[256,768]{1,0:T(8,128)(2,1)}, u32[]{:S(2)}, u32[]{:S(2)}) collective-permute-start(bf16[256,768]{1,0:T(8,128)(2,1)} %get-tuple-element.81), channel_id=1, source_target_pairs={{0,0},{1,2},{2,1},{3,3},{4,4},{5,6},{6,5},{7,7},{8,8},{9,10},{10,9... | collective-permute-start | bytes 1179656 | tf_op jit(solution)/shard_map/ppermute | solution.py:200
  105.2 100.9 %collective-permute-start.19 = (bf16[768,3072]{1,0:T(8,128)(2,1)}, bf16[768,3072]{1,0:T(8,128)(2,1)}, u32[]{:S(2)}, u32[]{:S(2)}) collective-permute-start(bf16[768,3072]{1,0:T(8,128)(2,1)} %pad_maximum_fusion), channel_id=1, source_target_pairs={{0,1},{1,0},{2,3},{3,2},{4,5},{5,4},{6,7},{7,6},{8,9},{9,8},{10,11... | collective-permute-start | bytes 14155784 | tf_op jit(solution)/shard_map/ppermute | solution.py:125
  340.4 61.7 %collective-permute-start.43 = (bf16[4992,768]{1,0:T(8,128)(2,1)}, bf16[4992,768]{1,0:T(8,128)(2,1)}, u32[]{:S(2)}, u32[]{:S(2)}) collective-permute-start(bf16[4992,768]{1,0:T(8,128)(2,1)} %fusion.89), channel_id=1, source_target_pairs={{0,1},{1,0},{2,3},{3,2},{4,5},{5,4},{6,7},{7,6},{8,9},{9,8},{10,11... | collective-permute-start | bytes 23003144 | tf_op jit(solution)/shard_map/ppermute | solution.py:125
  352.8 36.8 %collective-permute-start.24 = (f32[512,1536]{0,1:T(8,128)}, f32[512,1536]{0,1:T(8,128)}, u32[]{:S(2)}, u32[]{:S(2)}) collective-permute-start(f32[512,1536]{0,1:T(8,128)} %broadcast_select_fusion), channel_id=1, source_target_pairs={{0,1},{1,0},{2,3},{3,2},{4,5},{5,4},{6,7},{7,6},{8,9},{9,8},{10,11... | collective-permute-start | bytes 9437192 | tf_op jit(solution)/shard_map/ppermute | solution.py:343
  360.8 225.6 %collective-permute-start.21 = (bf16[256,768]{1,0:T(8,128)(2,1)}, bf16[256,768]{1,0:T(8,128)(2,1)S(1)}, u32[]{:S(2)}, u32[]{:S(2)}) collective-permute-start(bf16[256,768]{1,0:T(8,128)(2,1)} %get-tuple-element.84), channel_id=1, source_target_pairs={{2,0},{0,1},{3,2},{1,3},{6,4},{4,5},{7,6},{5,7},{10,8},{8,9},{11,1... | collective-permute-start | bytes 1179656 | tf_op jit(solution)/shard_map/ppermute | solution.py:212
  360.8 235.4 %collective-permute-start.20 = (bf16[256,768]{1,0:T(8,128)(2,1)}, bf16[256,768]{1,0:T(8,128)(2,1)}, u32[]{:S(2)}, u32[]{:S(2)}) collective-permute-start(bf16[256,768]{1,0:T(8,128)(2,1)} %get-tuple-element.83), channel_id=1, source_target_pairs={{0,0},{1,2},{2,1},{3,3},{4,4},{5,6},{6,5},{7,7},{8,8},{9,10},{10,9... | collective-permute-start | bytes 1179656 | tf_op jit(solution)/shard_map/ppermute | solution.py:211
  439.5 46.5 %collective-permute-start.44 = (bf16[2,2,624,384]{3,2,1,0:T(8,128)(2,1)S(1)}, bf16[2,2,624,384]{3,2,1,0:T(8,128)(2,1)S(1)}, u32[]{:S(2)}, u32[]{:S(2)}) collective-permute-start(bf16[2,2,624,384]{3,2,1,0:T(8,128)(2,1)S(1)} %pad_maximum_fusion.3), channel_id=1, source_target_pairs={{0,32},{32,64},{64,96},{96,0},{1,33},{33,65},{65,97},{97,1},{2,34}... | collective-permute-start | bytes 5750792 | tf_op jit(solution)/shard_map/ppermute | solution.py:49
  441.1 45.2 %collective-permute-start.45 = (bf16[2,2,624,384]{3,2,1,0:T(8,128)(2,1)S(1)}, bf16[2,2,624,384]{3,2,1,0:T(8,128)(2,1)S(1)}, u32[]{:S(2)}, u32[]{:S(2)}) collective-permute-start(bf16[2,2,624,384]{3,2,1,0:T(8,128)(2,1)S(1)} %pad_maximum_fusion.4), channel_id=1, source_target_pairs={{0,96},{32,0},{64,32},{96,64},{1,97},{33,1},{65,33},{97,65},{2,98}... | collective-permute-start | bytes 5750792 | tf_op jit(solution)/shard_map/ppermute | solution.py:49
  444.3 72.5 %collective-permute-start.27 = (bf16[1152,768]{1,0:T(8,128)(2,1)S(1)}, bf16[1152,768]{1,0:T(8,128)(2,1)S(1)}, u32[]{:S(2)}, u32[]{:S(2)}) collective-permute-start(bf16[1152,768]{1,0:T(8,128)(2,1)S(1)} %fusion.87), channel_id=1, source_target_pairs={{0,1},{1,0},{2,3},{3,2},{4,5},{5,4},{6,7},{7,6},{8,9},{9,8},{10,11... | collective-permute-start | bytes 5308424 | tf_op jit(solution)/shard_map/ppermute | solution.py:125
  486.3 24.5 %collective-permute-start.47 = (bf16[2,624,384]{2,1,0:T(8,128)(2,1)S(1)}, bf16[2,624,384]{2,1,0:T(8,128)(2,1)S(1)}, u32[]{:S(2)}, u32[]{:S(2)}) collective-permute-start(bf16[2,624,384]{2,1,0:T(8,128)(2,1)S(1)} %fusion.28), channel_id=1, source_target_pairs={{0,32},{32,64},{64,96},{96,0},{1,33},{33,65},{65,97},{97,1},{2,34}... | collective-permute-start | bytes 2875400 | tf_op jit(solution)/shard_map/ppermute | solution.py:49
  486.6 24.4 %collective-permute-start.46 = (bf16[2,624,384]{2,1,0:T(8,128)(2,1)S(1)}, bf16[2,624,384]{2,1,0:T(8,128)(2,1)S(1)}, u32[]{:S(2)}, u32[]{:S(2)}) collective-permute-start(bf16[2,624,384]{2,1,0:T(8,128)(2,1)S(1)} %fusion.30), channel_id=1, source_target_pairs={{0,96},{32,0},{64,32},{96,64},{1,97},{33,1},{65,33},{97,65},{2,98}... | collective-permute-start | bytes 2875400 | tf_op jit(solution)/shard_map/ppermute | solution.py:49
  586.4 31.1 %collective-permute-start.26 = (bf16[256,768]{1,0:T(8,128)(2,1)}, bf16[256,768]{1,0:T(8,128)(2,1)}, u32[]{:S(2)}, u32[]{:S(2)}) collective-permute-start(bf16[256,768]{1,0:T(8,128)(2,1)} %get-tuple-element.80), channel_id=1, source_target_pairs={{2,0},{0,1},{3,2},{1,3},{6,4},{4,5},{7,6},{5,7},{10,8},{8,9},{11,1... | collective-permute-start | bytes 1179656 | tf_op jit(solution)/shard_map/ppermute | solution.py:212
  586.5 31.0 %collective-permute-start.25 = (bf16[256,768]{1,0:T(8,128)(2,1)}, bf16[256,768]{1,0:T(8,128)(2,1)}, u32[]{:S(2)}, u32[]{:S(2)}) collective-permute-start(bf16[256,768]{1,0:T(8,128)(2,1)} %get-tuple-element.79), channel_id=1, source_target_pairs={{0,0},{1,2},{2,1},{3,3},{4,4},{5,6},{6,5},{7,7},{8,8},{9,10},{10,9... | collective-permute-start | bytes 1179656 | tf_op jit(solution)/shard_map/ppermute | solution.py:211
  591.0 44.0 %collective-permute-start.59 = (bf16[624,768]{1,0:T(8,128)(2,1)S(1)}, bf16[624,768]{1,0:T(8,128)(2,1)S(1)}, u32[]{:S(2)}, u32[]{:S(2)}) collective-permute-start(bf16[624,768]{1,0:T(8,128)(2,1)S(1)} %dynamic_update_slice.219), channel_id=1, source_target_pairs={{0,32},{32,64},{64,96},{96,0},{1,33},{33,65},{65,97},{97,1},{2,34}... | collective-permute-start | bytes 2875400 | tf_op jit(solution)/shard_map/ppermute | solution.py:49
  591.1 41.3 %collective-permute-start.60 = (bf16[624,768]{1,0:T(8,128)(2,1)S(1)}, bf16[624,768]{1,0:T(8,128)(2,1)S(1)}, u32[]{:S(2)}, u32[]{:S(2)}) collective-permute-start(bf16[624,768]{1,0:T(8,128)(2,1)S(1)} %dynamic_update_slice.219), channel_id=1, source_target_pairs={{0,96},{32,0},{64,32},{96,64},{1,97},{33,1},{65,33},{97,65},{2,98}... | collective-permute-start | bytes 2875400 | tf_op jit(solution)/shard_map/ppermute | solution.py:49
  (135 other events, 1476.8 us)

commit v3 on v2

--- a/solution.py
+++ b/solution.py
@@ -143,22 +143,15 @@
     return [own, partner[:rows], other, partner[rows:]]
 
 
-def gather_weights(shards, sizes):
-    w_query, w_key, w_value, w_out, w_gate, w_up, w_down = shards
-    plan = (
-        ((w_query, w_key, w_value), "y", True),
-        ((w_out, w_down), "z", False),
-        ((w_gate, w_up), "y", False),
-    )
-    out = {}
-    for group, axis, direct in plan:
-        parts = gather_group(jnp.concatenate(group), axis, sizes[axis], direct)
-        start = 0
-        for s in group:
-            rows = s.shape[0]
-            out[id(s)] = absolute([p[start:start + rows] for p in parts], rows)
-            start += rows
-    return [out[id(s)] for s in shards]
+def gather_weights(group, axis, sizes, direct):
+    parts = gather_group(jnp.concatenate(group), axis, sizes[axis], direct)
+    out = []
+    start = 0
+    for s in group:
+        rows = s.shape[0]
+        out.append(absolute([p[start:start + rows] for p in parts], rows))
+        start += rows
+    return out
 
 
 def reduce_group(grads, sizes, direct):
@@ -233,9 +226,8 @@
     cosine = jnp.cos(angles)[:, None, :]
     sine = jnp.sin(angles)[:, None, :]
 
-    shards = (w_query, w_key, w_value, w_out, w_gate, w_up, w_down)
-    query_weight, key_weight, value_weight, out_weight, gate_weight, up_weight, down_weight = (
-        gather_weights(shards, sizes)
+    query_weight, key_weight, value_weight = gather_weights(
+        (w_query, w_key, w_value), "y", sizes, True
     )
 
     hidden = to_sequence(tokens).astype(jnp.float32)
@@ -264,6 +256,9 @@
         .astype(jnp.bfloat16)
     )
     values = matmul(normed_low, value_weight).astype(jnp.bfloat16)
+    w_out, w_down, w_gate, w_up, values = lax.optimization_barrier((w_out, w_down, w_gate, w_up, values))
+    out_weight, down_weight = gather_weights((w_out, w_down), "z", sizes, False)
+    gate_weight, up_weight = gather_weights((w_gate, w_up), "y", sizes, False)
     both = swap_halves(jnp.concatenate([keys, values], axis=1))
     def heads(x, length):
         return x.reshape(length, head_count, head_size).transpose(1, 0, 2)
@@ -338,6 +333,10 @@
         jnp.einsum("hqk,hqd->hkd", probs_low, mixed_major, preferred_element_type=jnp.float32)
     )
     grad_kv = jnp.concatenate([grad_keys, grad_values], axis=1)
+    early = reduce_group(
+        [grads[6], grads[4].reshape(-1, width), grads[5].reshape(-1, width), grads[3]], sizes, False
+    )
+    early, grad_kv = lax.optimization_barrier((early, grad_kv))
     mine_kv = jnp.where(c == 0, grad_kv[:local_length], grad_kv[local_length:])
     theirs_kv = jnp.where(c == 0, grad_kv[local_length:], grad_kv[:local_length])
     own_kv = mine_kv + lax.ppermute(theirs_kv, "c", [(0, 1), (1, 0)])
@@ -362,16 +361,12 @@
     )
     grad_hidden = grad_after + norm_one_back(grad_normed)[0]
     input_grads = from_sequence(grad_hidden.astype(jnp.bfloat16))
-
-    width = grads[6].shape[1]
+    late = reduce_group([grads[0], grads[1], grads[2]], sizes, True)
     gate_rows = grads[4].shape[0]
-    early = reduce_group(
-        [grads[6], grads[4].reshape(-1, width), grads[5].reshape(-1, width), grads[3]], sizes, False
-    )
-    late = reduce_group([grads[0], grads[1], grads[2]], sizes, True)
     gate_grad = early[1].reshape(gate_rows // 4, -1)
     up_grad = early[2].reshape(gate_rows // 4, -1)
     owned = [late[0], late[1], late[2], early[3], gate_grad, up_grad, early[0]]
+
     return (output, input_grads, *owned)
 
 

time: 669 us -> 658 us (0.984)
  local copies, waits for them, and re-layouts: 143 us -> 129 us
    ppermute x2, starting transfers between devices: 9.16 us -> 1.36 us  [from_sequence(): first = lax.ppermute(first, GRP, [(0, 0), (1, 2), (2, 1), (3, 3)])]
    ppermute x2, starting transfers between devices: 0.09 us -> 7.56 us  [from_sequence(): second = lax.ppermute(second, GRP, [(2, 0), (0, 1), (3, 2), (1, 3)])]
    unnamed x204 -> x174, local copies, waits for them, and re-layouts: 36.3 us -> 32 us
    dynamic_update_slice x47 -> x48, local copies, waits for them, and re-layouts: 36.1 us -> 36.6 us  [place(): return lax.dynamic_update_slice(buf, piece, start)]
  transfers between devices with their start and end apart: 63 -> 63, of which waited for: 27 -> 27; matrix products, arithmetic and copies ran while one was open for 37% -> 36% of each run, Pallas kernels for 0% -> 0%
where the time goes in v3:
time: 658 us; the launch traced here: 647 us
  waiting for transfers between devices  160 us (24%)
  matrix products  141 us (21%)
  local copies, waits for them, and re-layouts  129 us (20%)
  other arithmetic  116 us (18%)
  starting transfers between devices  98 us (15%)
    ppermute x39, waiting for transfers between devices, shift(): return lax.ppermute(x, axis, [(i, (i + step) % n) for i in range(n)])  145 us
    ppermute x39, starting transfers between devices, shift(): return lax.ppermute(x, axis, [(i, (i + step) % n) for i in range(n)])  63.2 us
    dynamic_update_slice x48, local copies, waits for them, and re-layouts, place(): return lax.dynamic_update_slice(buf, piece, start)  36.6 us
    unnamed x174, local copies, waits for them, and re-layouts  32 us
    sub x1, matrix products, body(): grad_probs - inner  31.1 us
    dot_general x7, matrix products, matmul(): return jnp.dot(left, right, preferred_element_type=jnp.float32)  25.9 us
    another operation x3, other arithmetic, reduce_group(): pair = jnp.stack([own, oth])  22.2 us
    dot_general x7, matrix products, contract_cols(): lax.dot_general(left, right, (((1,), (1,)), ((), ())), preferred_element_...  19.5 us
  transfers between devices with their start and end apart: 63, of which 27 were waited for; matrix products, arithmetic and copies ran while one was open for 36% of the time, Pallas kernels for 0%

profile of v3, /device:TPU:0, one launch (start us, length us, event | category | flops | bytes accessed | tf_op | source)
XLA Modules:
  0.0 646.7 jit_solution(16827051052128468756)
XLA Ops:
  70.7 5.9 collective-permute-done.8
  102.7 6.7 %collective-permute-done.17 = bf16[48,3072]{1,0:T(8,128)(2,1)S(1)} collective-permute-done((bf16[48,3072]{1,0:T(8,128)(2,1)S(1)}, bf16[48,3072]{1,0:T(8,128)(2,1)S(1)}, u32[]{:S(2)}, u32[]{:S(2)}) %collective-permute-start.17) | collective-permute-done | bytes 294944 | tf_op jit(solution)/shard_map/ppermute | solution.py:49
  112.8 12.2 %maximum_select_fusion = bf16[1024,1536]{1,0:T(8,128)(2,1)S(1)} fusion(bf16[512,1536]{1,0:T(8,128)(2,1)S(1)} %collective-permute-done.7, bf16[512,768]{1,0:T(8,128)(2,1)S(1)} %copy-done.35, bf16[512,768]{1,0:T(8,128)(2,1)S(1)} %copy-done.25, pred[]{:T(512)S(6)} %eq.99), kind=kLoop, calls=%fused_computation.56 | loop fusion | flops 20447232 | bytes 6291457 | tf_op jit(solution)/shard_map/jit(_where)/select_n | solution.py:240
  129.5 14.3 %fusion.5 = (f32[12,512]{1,0:T(8,128)S(1)}, f32[12,512,1024]{2,1,0:T(8,128)}) fusion(pred[512,1024]{1,0:T(8,128)(4,1)} %fusion.22, bf16[12,1024,64]{1,2,0:T(8,128)(2,1)} %bitcast.198, bf16[512,12,32]{0,2,1:T(8,128)(2,1)} %get-tuple-element.86, bf16[512,12,32]{0,2,1:T(8,128)(2,1)S(1)} %get-tuple-element.85), kind=kOutput, calls=%fused_computation.19 | convolution fusion | flops 825747456 | bytes 28073984 | tf_op jit(solution)/shard_map/hqd,hkd->hqk/dot_general | solution.py:279
  143.8 12.6 %fusion.2 = f32[12,512]{1,0:T(8,128)S(1)} fusion(f32[12,512,1024]{2,1,0:T(8,128)} %get-tuple-element.119, f32[12,512]{1,0:T(8,128)S(1)} %get-tuple-element.118, pred[512,1024]{1,0:T(8,128)(4,1)S(1)} %copy-done.23), kind=kLoop, calls=%fused_computation.18 | loop fusion | flops 25159680 | bytes 25739264 | tf_op jit(solution)/shard_map/reduce_sum | solution.py:285
  159.2 8.8 %divide_convert_fusion = bf16[12,512,1024]{2,1,0:T(8,128)(2,1)} fusion(f32[12,512,1024]{2,1,0:T(8,128)S(1)} %copy-done, f32[12,512]{1,0:T(8,128)S(1)} %fusion.2, f32[12,512]{1,0:T(8,128)S(1)} %get-tuple-element.118, pred[512,1024]{1,0:T(8,128)(4,1)S(1)} %copy-done.23), kind=kLoop, calls=%fused_computation.15 | loop fusion | flops 31457280 | bytes 38322176 | tf_op jit(solution)/shard_map/convert_element_type | solution.py:287
  170.6 9.8 %convolution_convert_fusion.2 = bf16[12,512,64]{1,2,0:T(8,128)(2,1)} fusion(bf16[12,512,1024]{2,1,0:T(8,128)(2,1)} %divide_convert_fusion, bf16[12,1024,64]{1,2,0:T(8,128)(2,1)} %bitcast.214), kind=kOutput, calls=%fused_computation.120 | convolution fusion | flops 805699584 | bytes 14942208 | tf_op jit(solution)/shard_map/hqk,hkd->hqd/dot_general | solution.py:289
  192.3 7.8 %fusion.109 = f32[512,3072]{1,0:T(8,128)} fusion(bf16[3072,768]{1,0:T(8,128)(2,1)S(1)} %slice_dynamic-update-slice_fusion, bf16[256,768]{1,0:T(8,128)(2,1)} %collective-permute-done.23, bf16[256,768]{1,0:T(8,128)(2,1)} %collective-permute-done.22, pred[]{:T(512)S(6)} %eq.100), kind=kOutput, calls=%fused_computation.342 | convolution fusion | flops 2419458048 | bytes 11796481 | tf_op jit(solution)/shard_map/dot_general | solution.py:43
  207.8 9.4 %add_convert_fusion = (bf16[512,3072]{1,0:T(8,128)(2,1)S(1)}, bf16[512,3072]{1,0:T(8,128)(2,1)S(1)}, bf16[512,3072]{1,0:T(8,128)(2,1)}) fusion(f32[512,3072]{1,0:T(8,128)} %fusion.109, f32[512,3072]{1,0:T(8,128)S(1)} %fusion.116, bf16[512,768]{1,0:T(8,128)(2,1)S(1)} %multiply_convert_fusion.3, bf16[768,3072]{1,0:T(8,128)(2,1)S(1)} %get-tuple-element.49), kind=kOutput, calls=%fused_computation.40 | convolution fusion | flops 2444230656 | bytes 27525120 | tf_op jit(solution)/shard_map/dot_general | solution.py:33
  236.9 11.6 %reshape.310 = f32[3072,768]{1,0:T(8,128)} reshape(f32[768,3072]{1,0:T(8,128)} %fusion.120) | data formatting | bytes 18874368 | tf_op jit(solution)/shard_map/reshape | solution.py:337
  248.5 11.9 %reshape.309 = f32[3072,768]{1,0:T(8,128)} reshape(f32[768,3072]{1,0:T(8,128)} %fusion.119) | data formatting | bytes 18874368 | tf_op jit(solution)/shard_map/reshape | solution.py:337
  294.8 9.8 %convert_element_type.270 = f32[4992,768]{1,0:T(8,128)} convert(bf16[4992,768]{1,0:T(8,128)(2,1)} %collective-permute-done.24) | non-fusion elementwise | flops 3833856 | bytes 23003136 | tf_op jit(solution)/shard_map/convert_element_type | solution.py:165
  304.6 15.4 %fusion.10 = (f32[1,2496,768]{2,1,0:T(8,128)}, f32[1,2496,768]{2,1,0:T(8,128)}) fusion(f32[4992,768]{1,0:T(8,128)} %convert_element_type.270, f32[192,768]{1,0:T(8,128)S(1)} %copy-done.41, f32[768,768]{1,0:T(8,128)S(1)} %get-tuple-element.47, f32[768,768]{1,0:T(8,128)} %get-tuple-element.45, f32[768,768]{1,0:T(8,128)} %get-tuple-element.43, ...), kind=kLoop, calls=%fused_computation.25 | loop fusion | flops 15335424 | bytes 46006272 | tf_op jit(solution)/shard_map/stack | solution.py:169
  320.0 6.3 fusion.14
  333.9 41.0 %collective-permute-done.26 = bf16[2,2,624,384]{3,2,1,0:T(8,128)(2,1)S(1)} collective-permute-done((bf16[2,2,624,384]{3,2,1,0:T(8,128)(2,1)S(1)}, bf16[2,2,624,384]{3,2,1,0:T(8,128)(2,1)S(1)}, u32[]{:S(2)}, u32[]{:S(2)}) %collective-permute-start.26) | collective-permute-done | bytes 1916960 | tf_op jit(solution)/shard_map/ppermute | solution.py:49
  381.4 18.8 %collective-permute-done.27 = bf16[2,624,384]{2,1,0:T(8,128)(2,1)} collective-permute-done((bf16[2,624,384]{2,1,0:T(8,128)(2,1)}, bf16[2,624,384]{2,1,0:T(8,128)(2,1)}, u32[]{:S(2)}, u32[]{:S(2)}) %collective-permute-start.27) | collective-permute-done | bytes 958496 | tf_op jit(solution)/shard_map/ppermute | solution.py:49
  413.0 8.7 %collective-permute-done.30 = bf16[2,2,156,384]{3,2,1,0:T(8,128)(2,1)S(1)} collective-permute-done((bf16[2,2,156,384]{3,2,1,0:T(8,128)(2,1)S(1)}, bf16[2,2,156,384]{3,2,1,0:T(8,128)(2,1)S(1)}, u32[]{:S(2)}, u32[]{:S(2)}) %collective-permute-start.30) | collective-permute-done | bytes 479264 | tf_op jit(solution)/shard_map/ppermute | solution.py:49
  457.0 31.1 %multiply_convert_fusion = bf16[12,512,1024]{2,1,0:T(8,128)(2,1)} fusion(f32[12,512,1024]{2,1,0:T(8,128)} %get-tuple-element.119, f32[12,512]{1,0:T(8,128)S(1)} %log_add_fusion, pred[512,1024]{1,0:T(8,128)(4,1)S(1)} %copy-done.24, bf16[12,512,64]{1,2,0:T(8,128)(2,1)S(1)} %bitcast.207, bf16[12,1024,64]{1,2,0:T(8,128)(2,1)} %bitcast.215), kind=kOutput, calls=%fused_computation.11 | convolution fusion | flops 1679825920 | bytes 40656896 | tf_op jit(solution)/shard_map/sub | solution.py:325
  498.1 6.9 %fusion.62 = f32[12,1024,64]{1,2,0:T(8,128)S(1)} fusion(bf16[12,512,1024]{2,1,0:T(8,128)(2,1)} %multiply_convert_fusion, bf16[512,12,32]{0,2,1:T(8,128)(2,1)S(1)} %copy-done.34, bf16[512,12,32]{0,2,1:T(8,128)(2,1)S(1)} %copy-done.33), kind=kOutput, calls=%fused_computation.195 | convolution fusion | flops 806879232 | bytes 16515072 | tf_op jit(solution)/shard_map/hqk,hqd->hkd/dot_general | solution.py:330
  505.0 6.9 %fusion.125 = f32[12,1024,64]{1,2,0:T(8,128)S(1)} fusion(bf16[12,512,64]{1,2,0:T(8,128)(2,1)S(1)} %bitcast.208, bf16[12,512,1024]{2,1,0:T(8,128)(2,1)} %divide_convert_fusion), kind=kOutput, calls=%fused_computation.358 | convolution fusion | flops 805306368 | bytes 16515072 | tf_op jit(solution)/shard_map/hqk,hqd->hkd/dot_general | solution.py:333
  531.7 6.9 %add_convert_fusion.2 = bf16[512,768]{1,0:T(8,128)(2,1)} fusion(f32[512,768]{1,0:T(8,128)S(1)} %copy-done.4, bf16[512,3072]{1,0:T(8,128)(2,1)} %get-tuple-element.42, bf16[3072,768]{1,0:T(8,128)(2,1)} %copy-done.29), kind=kOutput, calls=%fused_computation.111 | convolution fusion | flops 2416705536 | bytes 10223616 | tf_op jit(solution)/shard_map/dot_general | solution.py:33
  538.6 8.5 %convolution_bitcast_fusion = f32[512,12,64]{0,2,1:T(8,128)S(1)} fusion(bf16[12,512,1024]{2,1,0:T(8,128)(2,1)} %multiply_convert_fusion, bf16[12,1024,64]{1,2,0:T(8,128)(2,1)S(1)} %bitcast.199), kind=kOutput, calls=%fused_computation.114 | convolution fusion | flops 805306368 | bytes 15728640 | tf_op jit(solution)/shard_map/hqk,hkd->hqd/dot_general | solution.py:327
  573.7 8.2 %collective-permute-done.48 = bf16[2,144,768]{2,1,0:T(8,128)(2,1)S(1)} collective-permute-done((bf16[2,144,768]{2,1,0:T(8,128)(2,1)S(1)}, bf16[2,144,768]{2,1,0:T(8,128)(2,1)S(1)}, u32[]{:S(2)}, u32[]{:S(2)}) %collective-permute-start.48) | collective-permute-done | bytes 442400 | tf_op jit(solution)/shard_map/ppermute | solution.py:49
  581.9 10.7 %collective-permute-done.49 = bf16[2,144,768]{2,1,0:T(8,128)(2,1)S(1)} collective-permute-done((bf16[2,144,768]{2,1,0:T(8,128)(2,1)S(1)}, bf16[2,144,768]{2,1,0:T(8,128)(2,1)S(1)}, u32[]{:S(2)}, u32[]{:S(2)}) %collective-permute-start.49) | collective-permute-done | bytes 442400 | tf_op jit(solution)/shard_map/ppermute | solution.py:49
  (485 shorter events, 353.8 us)
Async XLA Ops:
  7.5 33.2 %collective-permute-start = (bf16[256,768]{1,0:T(8,128)(2,1)}, bf16[256,768]{1,0:T(8,128)(2,1)S(1)}, u32[]{:S(2)}, u32[]{:S(2)}) collective-permute-start(bf16[256,768]{1,0:T(8,128)(2,1)} %get-tuple-element.106), channel_id=1, source_target_pairs={{0,0},{1,2},{2,1},{3,3},{4,4},{5,6},{6,5},{7,7},{8,8},{9,10},{10,9... | collective-permute-start | bytes 1179656 | tf_op jit(solution)/shard_map/ppermute | solution.py:193
  9.1 31.6 %collective-permute-start.1 = (bf16[256,768]{1,0:T(8,128)(2,1)}, bf16[256,768]{1,0:T(8,128)(2,1)S(1)}, u32[]{:S(2)}, u32[]{:S(2)}) collective-permute-start(bf16[256,768]{1,0:T(8,128)(2,1)} %get-tuple-element.105), channel_id=1, source_target_pairs={{0,2},{1,0},{2,3},{3,1},{4,6},{5,4},{6,7},{7,5},{8,10},{9,8},{10,1... | collective-permute-start | bytes 1179656 | tf_op jit(solution)/shard_map/ppermute | solution.py:194
  13.1 179.2 %collective-permute-start.22 = (bf16[256,768]{1,0:T(8,128)(2,1)}, bf16[256,768]{1,0:T(8,128)(2,1)}, u32[]{:S(2)}, u32[]{:S(2)}) collective-permute-start(bf16[256,768]{1,0:T(8,128)(2,1)} %get-tuple-element.101), channel_id=1, source_target_pairs={{0,0},{1,2},{2,1},{3,3},{4,4},{5,6},{6,5},{7,7},{8,8},{9,10},{10,9... | collective-permute-start | bytes 1179656 | tf_op jit(solution)/shard_map/ppermute | solution.py:193
  51.4 30.6 %collective-permute-start.14 = (bf16[96,3072]{1,0:T(8,128)(2,1)}, bf16[96,3072]{1,0:T(8,128)(2,1)}, u32[]{:S(2)}, u32[]{:S(2)}) collective-permute-start(bf16[96,3072]{1,0:T(8,128)(2,1)} %fusion.61), channel_id=1, source_target_pairs={{0,6},{2,4},{4,2},{6,0},{1,7},{3,5},{5,3},{7,1},{8,14},{10,12},{12... | collective-permute-start | bytes 1769480 | tf_op jit(solution)/shard_map/ppermute | solution.py:121
  54.6 22.0 %collective-permute-start.8 = (bf16[240,768]{1,0:T(8,128)(2,1)}, bf16[240,768]{1,0:T(8,128)(2,1)}, u32[]{:S(2)}, u32[]{:S(2)}) collective-permute-start(bf16[240,768]{1,0:T(8,128)(2,1)} %fusion.78), channel_id=1, source_target_pairs={{0,6},{2,4},{4,2},{6,0},{1,7},{3,5},{5,3},{7,1},{8,14},{10,12},{12... | collective-permute-start | bytes 1105928 | tf_op jit(solution)/shard_map/ppermute | solution.py:121
  82.0 17.1 %collective-permute-start.15 = (bf16[96,3072]{1,0:T(8,128)(2,1)}, bf16[96,3072]{1,0:T(8,128)(2,1)S(1)}, u32[]{:S(2)}, u32[]{:S(2)}) collective-permute-start(bf16[96,3072]{1,0:T(8,128)(2,1)} %collective-permute-done.14), channel_id=1, source_target_pairs={{0,32},{32,64},{64,96},{96,0},{1,33},{33,65},{65,97},{97,1},{2,34}... | collective-permute-start | bytes 1769480 | tf_op jit(solution)/shard_map/ppermute | solution.py:49
  82.1 17.2 %collective-permute-start.16 = (bf16[96,3072]{1,0:T(8,128)(2,1)}, bf16[96,3072]{1,0:T(8,128)(2,1)S(1)}, u32[]{:S(2)}, u32[]{:S(2)}) collective-permute-start(bf16[96,3072]{1,0:T(8,128)(2,1)} %collective-permute-done.14), channel_id=1, source_target_pairs={{0,96},{32,0},{64,32},{96,64},{1,97},{33,1},{65,33},{97,65},{2,98}... | collective-permute-start | bytes 1769480 | tf_op jit(solution)/shard_map/ppermute | solution.py:49
  96.5 95.8 %collective-permute-start.23 = (bf16[256,768]{1,0:T(8,128)(2,1)}, bf16[256,768]{1,0:T(8,128)(2,1)}, u32[]{:S(2)}, u32[]{:S(2)}) collective-permute-start(bf16[256,768]{1,0:T(8,128)(2,1)} %get-tuple-element.102), channel_id=1, source_target_pairs={{0,2},{1,0},{2,3},{3,1},{4,6},{5,4},{6,7},{7,5},{8,10},{9,8},{10,1... | collective-permute-start | bytes 1179656 | tf_op jit(solution)/shard_map/ppermute | solution.py:194
  109.4 71.0 %collective-permute-start.13 = (bf16[1920,768]{1,0:T(8,128)(2,1)}, bf16[1920,768]{1,0:T(8,128)(2,1)}, u32[]{:S(2)}, u32[]{:S(2)}) collective-permute-start(bf16[1920,768]{1,0:T(8,128)(2,1)} %pad_maximum_fusion.2), channel_id=1, source_target_pairs={{0,1},{1,0},{2,3},{3,2},{4,5},{5,4},{6,7},{7,6},{8,9},{9,8},{10,11... | collective-permute-start | bytes 8847368 | tf_op jit(solution)/shard_map/ppermute | solution.py:125
  111.9 88.3 %collective-permute-start.19 = (bf16[768,3072]{1,0:T(8,128)(2,1)}, bf16[768,3072]{1,0:T(8,128)(2,1)}, u32[]{:S(2)}, u32[]{:S(2)}) collective-permute-start(bf16[768,3072]{1,0:T(8,128)(2,1)} %pad_maximum_fusion.1), channel_id=1, source_target_pairs={{0,1},{1,0},{2,3},{3,2},{4,5},{5,4},{6,7},{7,6},{8,9},{9,8},{10,11... | collective-permute-start | bytes 14155784 | tf_op jit(solution)/shard_map/ppermute | solution.py:125
  330.6 44.3 %collective-permute-start.26 = (bf16[2,2,624,384]{3,2,1,0:T(8,128)(2,1)S(1)}, bf16[2,2,624,384]{3,2,1,0:T(8,128)(2,1)S(1)}, u32[]{:S(2)}, u32[]{:S(2)}) collective-permute-start(bf16[2,2,624,384]{3,2,1,0:T(8,128)(2,1)S(1)} %pad_maximum_fusion.4), channel_id=1, source_target_pairs={{0,96},{32,0},{64,32},{96,64},{1,97},{33,1},{65,33},{97,65},{2,98}... | collective-permute-start | bytes 5750792 | tf_op jit(solution)/shard_map/ppermute | solution.py:49
  333.8 46.0 %collective-permute-start.25 = (bf16[2,2,624,384]{3,2,1,0:T(8,128)(2,1)S(1)}, bf16[2,2,624,384]{3,2,1,0:T(8,128)(2,1)S(1)}, u32[]{:S(2)}, u32[]{:S(2)}) collective-permute-start(bf16[2,2,624,384]{3,2,1,0:T(8,128)(2,1)S(1)} %pad_maximum_fusion.3), channel_id=1, source_target_pairs={{0,32},{32,64},{64,96},{96,0},{1,33},{33,65},{65,97},{97,1},{2,34}... | collective-permute-start | bytes 5750792 | tf_op jit(solution)/shard_map/ppermute | solution.py:49
  376.1 24.1 %collective-permute-start.27 = (bf16[2,624,384]{2,1,0:T(8,128)(2,1)}, bf16[2,624,384]{2,1,0:T(8,128)(2,1)}, u32[]{:S(2)}, u32[]{:S(2)}) collective-permute-start(bf16[2,624,384]{2,1,0:T(8,128)(2,1)} %fusion.29), channel_id=1, source_target_pairs={{0,96},{32,0},{64,32},{96,64},{1,97},{33,1},{65,33},{97,65},{2,98}... | collective-permute-start | bytes 2875400 | tf_op jit(solution)/shard_map/ppermute | solution.py:49
  381.4 23.8 %collective-permute-start.28 = (bf16[2,624,384]{2,1,0:T(8,128)(2,1)}, bf16[2,624,384]{2,1,0:T(8,128)(2,1)}, u32[]{:S(2)}, u32[]{:S(2)}) collective-permute-start(bf16[2,624,384]{2,1,0:T(8,128)(2,1)} %fusion.27), channel_id=1, source_target_pairs={{0,32},{32,64},{64,96},{96,0},{1,33},{33,65},{65,97},{97,1},{2,34}... | collective-permute-start | bytes 2875400 | tf_op jit(solution)/shard_map/ppermute | solution.py:49
  452.7 40.5 %collective-permute-start.38 = (bf16[78,768]{1,0:T(8,128)(2,1)S(1)}, bf16[78,768]{1,0:T(8,128)(2,1)S(1)}, u32[]{:S(2)}, u32[]{:S(2)}) collective-permute-start(bf16[78,768]{1,0:T(8,128)(2,1)S(1)} %slice.450), channel_id=1, source_target_pairs={{0,8},{8,16},{16,24},{24,0},{1,9},{9,17},{17,25},{25,1},{2,10},{10... | collective-permute-start | bytes 359432 | tf_op jit(solution)/shard_map/ppermute | solution.py:49
  453.7 39.5 %collective-permute-start.39 = (bf16[78,768]{1,0:T(8,128)(2,1)S(1)}, bf16[78,768]{1,0:T(8,128)(2,1)S(1)}, u32[]{:S(2)}, u32[]{:S(2)}) collective-permute-start(bf16[78,768]{1,0:T(8,128)(2,1)S(1)} %slice.451), channel_id=1, source_target_pairs={{0,24},{8,0},{16,8},{24,16},{1,25},{9,1},{17,9},{25,17},{2,26},{10... | collective-permute-start | bytes 359432 | tf_op jit(solution)/shard_map/ppermute | solution.py:49
  494.6 20.1 %collective-permute-start.40 = (bf16[624,768]{1,0:T(8,128)(2,1)S(1)}, bf16[624,768]{1,0:T(8,128)(2,1)S(1)}, u32[]{:S(2)}, u32[]{:S(2)}) collective-permute-start(bf16[624,768]{1,0:T(8,128)(2,1)S(1)} %dynamic_update_slice.211), channel_id=1, source_target_pairs={{0,32},{32,64},{64,96},{96,0},{1,33},{33,65},{65,97},{97,1},{2,34}... | collective-permute-start | bytes 2875400 | tf_op jit(solution)/shard_map/ppermute | solution.py:49
  494.7 20.1 %collective-permute-start.41 = (bf16[624,768]{1,0:T(8,128)(2,1)S(1)}, bf16[624,768]{1,0:T(8,128)(2,1)S(1)}, u32[]{:S(2)}, u32[]{:S(2)}) collective-permute-start(bf16[624,768]{1,0:T(8,128)(2,1)S(1)} %dynamic_update_slice.211), channel_id=1, source_target_pairs={{0,96},{32,0},{64,32},{96,64},{1,97},{33,1},{65,33},{97,65},{2,98}... | collective-permute-start | bytes 2875400 | tf_op jit(solution)/shard_map/ppermute | solution.py:49
  557.5 57.5 %collective-permute-start.20 = (bf16[256,768]{1,0:T(8,128)(2,1)S(1)}, bf16[256,768]{1,0:T(8,128)(2,1)S(1)}, u32[]{:S(2)}, u32[]{:S(2)}) collective-permute-start(bf16[256,768]{1,0:T(8,128)(2,1)S(1)} %get-tuple-element.103), channel_id=1, source_target_pairs={{0,0},{1,2},{2,1},{3,3},{4,4},{5,6},{6,5},{7,7},{8,8},{9,10},{10,9... | collective-permute-start | bytes 1179656 | tf_op jit(solution)/shard_map/ppermute | solution.py:204
  558.2 60.3 %collective-permute-start.21 = (bf16[256,768]{1,0:T(8,128)(2,1)S(1)}, bf16[256,768]{1,0:T(8,128)(2,1)S(1)}, u32[]{:S(2)}, u32[]{:S(2)}) collective-permute-start(bf16[256,768]{1,0:T(8,128)(2,1)S(1)} %get-tuple-element.104), channel_id=1, source_target_pairs={{2,0},{0,1},{3,2},{1,3},{6,4},{4,5},{7,6},{5,7},{10,8},{8,9},{11,1... | collective-permute-start | bytes 1179656 | tf_op jit(solution)/shard_map/ppermute | solution.py:205
  568.2 24.3 %collective-permute-start.49 = (bf16[2,144,768]{2,1,0:T(8,128)(2,1)S(1)}, bf16[2,144,768]{2,1,0:T(8,128)(2,1)S(1)}, u32[]{:S(2)}, u32[]{:S(2)}) collective-permute-start(bf16[2,144,768]{2,1,0:T(8,128)(2,1)S(1)} %get-tuple-element.62), channel_id=1, source_target_pairs={{0,64},{32,96},{64,0},{96,32},{1,65},{33,97},{65,1},{97,33},{2,66}... | collective-permute-start | bytes 1327112 | tf_op jit(solution)/shard_map/ppermute | solution.py:49
  573.0 19.6 %collective-permute-start.50 = (bf16[2,144,768]{2,1,0:T(8,128)(2,1)S(1)}, bf16[2,144,768]{2,1,0:T(8,128)(2,1)S(1)}, u32[]{:S(2)}, u32[]{:S(2)}) collective-permute-start(bf16[2,144,768]{2,1,0:T(8,128)(2,1)S(1)} %get-tuple-element.63), channel_id=1, source_target_pairs={{0,96},{32,0},{64,32},{96,64},{1,97},{33,1},{65,33},{97,65},{2,98}... | collective-permute-start | bytes 1327112 | tf_op jit(solution)/shard_map/ppermute | solution.py:49
  609.0 21.1 %collective-permute-start.45 = (bf16[256,768]{1,0:T(8,128)(2,1)S(1)}, bf16[256,768]{1,0:T(8,128)(2,1)S(1)}, u32[]{:S(2)}, u32[]{:S(2)}) collective-permute-start(bf16[256,768]{1,0:T(8,128)(2,1)S(1)} %get-tuple-element.99), channel_id=1, source_target_pairs={{0,0},{1,2},{2,1},{3,3},{4,4},{5,6},{6,5},{7,7},{8,8},{9,10},{10,9... | collective-permute-start | bytes 1179656 | tf_op jit(solution)/shard_map/ppermute | solution.py:204
  609.7 20.4 %collective-permute-start.46 = (bf16[256,768]{1,0:T(8,128)(2,1)S(1)}, bf16[256,768]{1,0:T(8,128)(2,1)}, u32[]{:S(2)}, u32[]{:S(2)}) collective-permute-start(bf16[256,768]{1,0:T(8,128)(2,1)S(1)} %get-tuple-element.100), channel_id=1, source_target_pairs={{2,0},{0,1},{3,2},{1,3},{6,4},{4,5},{7,6},{5,7},{10,8},{8,9},{11,1... | collective-permute-start | bytes 1179656 | tf_op jit(solution)/shard_map/ppermute | solution.py:205
  (120 other events, 1312.1 us)

commit v4 on v3

--- a/solution.py
+++ b/solution.py
@@ -227,11 +227,12 @@
     sine = jnp.sin(angles)[:, None, :]
 
     query_weight, key_weight, value_weight = gather_weights(
-        (w_query, w_key, w_value), "y", sizes, True
-    )
-
-    hidden = to_sequence(tokens).astype(jnp.float32)
-    grad_result = to_sequence(cotangent)
+        (w_query, w_key, w_value), "y", {"y": 1}, True
+    )
+
+    both_in = to_sequence(jnp.concatenate([tokens, cotangent], axis=2))
+    hidden = both_in[:, :width].astype(jnp.float32)
+    grad_result = both_in[:, width:]
     seg_row = lax.dynamic_index_in_dim(segment, xh, 0, False)
     start_row = lax.dynamic_index_in_dim(piece_start, xh, 0, False)
 
@@ -257,8 +258,13 @@
     )
     values = matmul(normed_low, value_weight).astype(jnp.bfloat16)
     w_out, w_down, w_gate, w_up, values = lax.optimization_barrier((w_out, w_down, w_gate, w_up, values))
-    out_weight, down_weight = gather_weights((w_out, w_down), "z", sizes, False)
-    gate_weight, up_weight = gather_weights((w_gate, w_up), "y", sizes, False)
+    width_of_gate = w_gate.shape[1]
+    folded = [w.reshape(-1, width) for w in (w_gate, w_up)]
+    out_weight, down_weight, gate_weight, up_weight = gather_weights(
+        (w_out, w_down, folded[0], folded[1]), "y", sizes, False
+    )
+    gate_weight = gate_weight.reshape(-1, width_of_gate)
+    up_weight = up_weight.reshape(-1, width_of_gate)
     both = swap_halves(jnp.concatenate([keys, values], axis=1))
     def heads(x, length):
         return x.reshape(length, head_count, head_size).transpose(1, 0, 2)
@@ -297,7 +303,7 @@
     active, gate_back = jax.vjp(gated, gate, upper)
     active_low = active.astype(jnp.bfloat16)
     result = after + matmul(active_low, down_weight)
-    output = from_sequence(result.astype(jnp.bfloat16))
+    result_low = result.astype(jnp.bfloat16)
 
     grads = [None] * 7
     grads[6] = contract_rows(active_low, grad_result)
@@ -305,8 +311,13 @@
     grad_gate, grad_upper = gate_back(grad_active)
     gate_low = grad_gate.astype(jnp.bfloat16)
     upper_low = grad_upper.astype(jnp.bfloat16)
-    grads[4] = contract_rows(normed_two_low, gate_low)
-    grads[5] = contract_rows(normed_two_low, upper_low)
+    def folded_grad(left, right):
+        blocks = right.reshape(right.shape[0], -1, width)
+        out = jnp.einsum("td,tcf->dcf", left, blocks, preferred_element_type=jnp.float32)
+        return out.reshape(-1, width)
+
+    grads[4] = folded_grad(normed_two_low, gate_low)
+    grads[5] = folded_grad(normed_two_low, upper_low)
     grad_normed_two = contract_cols(gate_low, gate_weight) + contract_cols(upper_low, up_weight)
     grad_after = grad_result.astype(jnp.float32) + norm_two_back(grad_normed_two)[0]
     after_low = grad_after.astype(jnp.bfloat16)
@@ -333,10 +344,6 @@
         jnp.einsum("hqk,hqd->hkd", probs_low, mixed_major, preferred_element_type=jnp.float32)
     )
     grad_kv = jnp.concatenate([grad_keys, grad_values], axis=1)
-    early = reduce_group(
-        [grads[6], grads[4].reshape(-1, width), grads[5].reshape(-1, width), grads[3]], sizes, False
-    )
-    early, grad_kv = lax.optimization_barrier((early, grad_kv))
     mine_kv = jnp.where(c == 0, grad_kv[:local_length], grad_kv[local_length:])
     theirs_kv = jnp.where(c == 0, grad_kv[local_length:], grad_kv[:local_length])
     own_kv = mine_kv + lax.ppermute(theirs_kv, "c", [(0, 1), (1, 0)])
@@ -360,12 +367,12 @@
         + contract_cols(values_low, value_weight)
     )
     grad_hidden = grad_after + norm_one_back(grad_normed)[0]
-    input_grads = from_sequence(grad_hidden.astype(jnp.bfloat16))
-    late = reduce_group([grads[0], grads[1], grads[2]], sizes, True)
-    gate_rows = grads[4].shape[0]
-    gate_grad = early[1].reshape(gate_rows // 4, -1)
-    up_grad = early[2].reshape(gate_rows // 4, -1)
-    owned = [late[0], late[1], late[2], early[3], gate_grad, up_grad, early[0]]
+    both_out = from_sequence(jnp.concatenate([result_low, grad_hidden.astype(jnp.bfloat16)], axis=1))
+    output = both_out[..., :width]
+    input_grads = both_out[..., width:]
+    owned = reduce_group(grads, sizes, False)
+    owned[4] = owned[4].reshape(-1, width_of_gate)
+    owned[5] = owned[5].reshape(-1, width_of_gate)
 
     return (output, input_grads, *owned)
 

time: 658 us -> 698 us (1.061)
  the two profiles are of different devices: /device:TPU:0 before, /device:TPU:1 now
where the time goes in v4:
time: 698 us; the launch traced here: 686 us
  local copies, waits for them, and re-layouts  191 us (27%)
  waiting for transfers between devices  184 us (26%)
  matrix products  146 us (21%)
  other arithmetic  103 us (15%)
  starting transfers between devices  60.3 us (9%)
    ppermute x20, waiting for transfers between devices, shift(): return lax.ppermute(x, axis, [(i, (i + step) % n) for i in range(n)])  110 us
    unnamed x199, local copies, waits for them, and re-layouts  56.7 us
    ppermute x3, waiting for transfers between devices, cross(): return lax.ppermute(x, ('xl', 'xh'), [(i, 3 - i) for i in range(4)])  53.7 us
    sub x1, matrix products, body(): grad_probs - inner  31.5 us
    ppermute x20, starting transfers between devices, shift(): return lax.ppermute(x, axis, [(i, (i + step) % n) for i in range(n)])  29.8 us
    dynamic_update_slice x27, local copies, waits for them, and re-layouts, place(): return lax.dynamic_update_slice(buf, piece, start)  27.3 us
    dot_general x2, local copies, waits for them, and re-layouts, folded_grad(): jnp.einsum('td,tcf->dcf', left, blocks, preferred_element_type=jnp.float32)  26.6 us
    dot_general x7, matrix products, matmul(): return jnp.dot(left, right, preferred_element_type=jnp.float32)  26.6 us
  transfers between devices with their start and end apart: 34, of which 18 were waited for; matrix products, arithmetic and copies ran while one was open for 31% of the time, Pallas kernels for 0%

profile of v4, /device:TPU:1, one launch (start us, length us, event | category | flops | bytes accessed | tf_op | source)
XLA Modules:
  0.0 685.8 jit_solution(11513874133325522364)
XLA Ops:
  12.4 28.6 %collective-permute-done.2 = bf16[576,768]{1,0:T(8,128)(2,1)S(1)} collective-permute-done((bf16[576,768]{1,0:T(8,128)(2,1)S(1)}, bf16[576,768]{1,0:T(8,128)(2,1)S(1)}, u32[]{:S(2)}, u32[]{:S(2)}) %collective-permute-start.2) | collective-permute-done | bytes 884768 | tf_op jit(solution)/shard_map/ppermute | solution.py:121
  70.1 17.8 %collective-permute-done.5 = bf16[624,768]{1,0:T(8,128)(2,1)} collective-permute-done((bf16[624,768]{1,0:T(8,128)(2,1)S(1)}, bf16[624,768]{1,0:T(8,128)(2,1)}, u32[]{:S(2)}, u32[]{:S(2)}) %collective-permute-start.5) | collective-permute-done | bytes 958496 | tf_op jit(solution)/shard_map/ppermute | solution.py:121
  133.9 12.2 %maximum_select_fusion = bf16[1024,1536]{1,0:T(8,128)(2,1)S(1)} fusion(bf16[512,1536]{1,0:T(8,128)(2,1)S(1)} %collective-permute-done.4, bf16[512,768]{1,0:T(8,128)(2,1)S(1)} %copy-done.30, bf16[512,768]{1,0:T(8,128)(2,1)S(1)} %copy.34, pred[]{:T(512)S(6)} %eq.75), kind=kLoop, calls=%fused_computation.60 | loop fusion | flops 20447232 | bytes 6291457 | tf_op jit(solution)/shard_map/jit(_where)/select_n | solution.py:241
  149.8 12.5 %fusion.5 = (f32[12,512]{1,0:T(8,128)S(1)}, f32[12,512,1024]{2,1,0:T(8,128)}) fusion(pred[512,1024]{1,0:T(8,128)(4,1)} %fusion.37, bf16[12,1024,64]{1,2,0:T(8,128)(2,1)S(1)} %bitcast.181, bf16[512,12,32]{0,2,1:T(8,128)(2,1)} %get-tuple-element.80, bf16[512,12,32]{0,2,1:T(8,128)(2,1)S(1)} %copy-done.29), kind=kOutput, calls=%fused_computation.19 | convolution fusion | flops 825747456 | bytes 28073984 | tf_op jit(solution)/shard_map/hqd,hkd->hqk/dot_general | solution.py:285
  162.3 12.3 %fusion.2 = f32[12,512]{1,0:T(8,128)S(1)} fusion(f32[12,512,1024]{2,1,0:T(8,128)} %get-tuple-element.111, f32[12,512]{1,0:T(8,128)S(1)} %get-tuple-element.110, pred[512,1024]{1,0:T(8,128)(4,1)S(1)} %copy-done.17), kind=kLoop, calls=%fused_computation.18 | loop fusion | flops 25159680 | bytes 25739264 | tf_op jit(solution)/shard_map/reduce_sum | solution.py:291
  177.7 9.2 %divide_convert_fusion = bf16[12,512,1024]{2,1,0:T(8,128)(2,1)} fusion(f32[12,512,1024]{2,1,0:T(8,128)S(1)} %copy-done, f32[12,512]{1,0:T(8,128)S(1)} %fusion.2, f32[12,512]{1,0:T(8,128)S(1)} %get-tuple-element.110, pred[512,1024]{1,0:T(8,128)(4,1)S(1)} %copy-done.17), kind=kLoop, calls=%fused_computation.15 | loop fusion | flops 31457280 | bytes 38322176 | tf_op jit(solution)/shard_map/convert_element_type | solution.py:293
  189.9 9.9 %convolution_convert_fusion.2 = bf16[12,512,64]{1,2,0:T(8,128)(2,1)} fusion(bf16[12,512,1024]{2,1,0:T(8,128)(2,1)} %divide_convert_fusion, bf16[12,1024,64]{1,2,0:T(8,128)(2,1)} %bitcast.187), kind=kOutput, calls=%fused_computation.128 | convolution fusion | flops 805699584 | bytes 14942208 | tf_op jit(solution)/shard_map/hqk,hkd->hqd/dot_general | solution.py:295
  220.4 8.5 %reshape.335 = bf16[768,3072]{1,0:T(8,128)(2,1)} reshape(bf16[3072,768]{1,0:T(8,128)(2,1)} %get-tuple-element.42) | data formatting | bytes 9437184 | tf_op jit(solution)/shard_map/reshape | solution.py:266
  235.7 8.5 %reshape.336 = bf16[768,3072]{1,0:T(8,128)(2,1)} reshape(bf16[3072,768]{1,0:T(8,128)(2,1)} %get-tuple-element.39) | data formatting | bytes 9437184 | tf_op jit(solution)/shard_map/reshape | solution.py:267
  249.0 9.6 %multiply_convert_fusion.2 = (bf16[512,3072]{1,0:T(8,128)(2,1)}, bf16[512,3072]{1,0:T(8,128)(2,1)}, bf16[512,3072]{1,0:T(8,128)(2,1)S(1)}) fusion(f32[512,3072]{1,0:T(8,128)S(1)} %fusion.120, f32[512,3072]{1,0:T(8,128)} %fusion.80, bf16[512,768]{1,0:T(8,128)(2,1)S(1)} %copy-done.31, bf16[768,3072]{1,0:T(8,128)(2,1)S(1)} %copy-done.26), kind=kOutput, calls=%fused_computation.43 | convolution fusion | flops 2444230656 | bytes 27525120 | tf_op jit(solution)/shard_map/dot_general | solution.py:33
  270.5 8.6 %fusion.125 = f32[12,1024,64]{1,2,0:T(8,128)} fusion(bf16[12,512,64]{1,2,0:T(8,128)(2,1)S(1)} %bitcast.184, bf16[12,512,1024]{2,1,0:T(8,128)(2,1)} %divide_convert_fusion), kind=kOutput, calls=%fused_computation.327 | convolution fusion | flops 805306368 | bytes 16515072 | tf_op jit(solution)/shard_map/hqk,hqd->hkd/dot_general | solution.py:344
  279.1 31.5 %multiply_convert_fusion = bf16[12,512,1024]{2,1,0:T(8,128)(2,1)} fusion(f32[12,512,1024]{2,1,0:T(8,128)} %get-tuple-element.111, f32[12,512]{1,0:T(8,128)S(1)} %copy-done.71, pred[512,1024]{1,0:T(8,128)(4,1)S(1)} %copy-done.18, bf16[12,512,64]{1,2,0:T(8,128)(2,1)S(1)} %bitcast.185, bf16[12,1024,64]{1,2,0:T(8,128)(2,1)} %bitcast.188), kind=kOutput, calls=%fused_computation.11 | convolution fusion | flops 1679825920 | bytes 40656896 | tf_op jit(solution)/shard_map/sub | solution.py:336
  327.5 13.3 %copy.40 = f32[768,4,768]{2,1,0:T(4,128)} copy(f32[768,4,768]{2,0,1:T(8,128)} %fusion.19) | data formatting | bytes 18874368 | tf_op jit(solution)/shard_map/td,tcf->dcf/dot_general | solution.py:316
  340.8 12.0 %reshape.341 = f32[3072,768]{1,0:T(8,128)} reshape(f32[768,4,768]{2,1,0:T(4,128)} %copy.40) | data formatting | bytes 18874368 | tf_op jit(solution)/shard_map/reshape | solution.py:317
  359.9 13.3 %copy.43 = f32[768,4,768]{2,1,0:T(4,128)} copy(f32[768,4,768]{2,0,1:T(8,128)} %fusion.16) | data formatting | bytes 18874368 | tf_op jit(solution)/shard_map/td,tcf->dcf/dot_general | solution.py:316
  373.2 12.1 %reshape.343 = f32[3072,768]{1,0:T(8,128)} reshape(f32[768,4,768]{2,1,0:T(4,128)} %copy.43) | data formatting | bytes 18874368 | tf_op jit(solution)/shard_map/reshape | solution.py:317
  393.0 9.6 %convolution_bitcast_fusion = f32[512,12,64]{0,2,1:T(8,128)} fusion(bf16[12,512,1024]{2,1,0:T(8,128)(2,1)} %multiply_convert_fusion, bf16[12,1024,64]{1,2,0:T(8,128)(2,1)S(1)} %bitcast.182), kind=kOutput, calls=%fused_computation.121 | convolution fusion | flops 805306368 | bytes 15728640 | tf_op jit(solution)/shard_map/hqk,hkd->hqd/dot_general | solution.py:338
  456.7 11.5 %convert_element_type.213 = f32[6144,768]{1,0:T(8,128)} convert(bf16[6144,768]{1,0:T(8,128)(2,1)} %collective-permute-done.14) | non-fusion elementwise | flops 4718592 | bytes 28311552 | tf_op jit(solution)/shard_map/convert_element_type | solution.py:165
  468.2 12.8 %fusion.10 = (f32[1,3072,768]{2,1,0:T(8,128)S(1)}, f32[1,3072,768]{2,1,0:T(8,128)S(1)}) fusion(f32[3072,768]{1,0:T(8,128)} %get-tuple-element.33, f32[6144,768]{1,0:T(8,128)} %convert_element_type.213, f32[3072,768]{1,0:T(8,128)} %get-tuple-element.34), kind=kLoop, calls=%fused_computation.25 | loop fusion | flops 4718592 | bytes 56623104 | tf_op jit(solution)/shard_map/stack | solution.py:169
  487.7 50.5 %collective-permute-done.15 = bf16[2,2,768,384]{3,2,1,0:T(8,128)(2,1)S(1)} collective-permute-done((bf16[2,2,768,384]{3,2,1,0:T(8,128)(2,1)S(1)}, bf16[2,2,768,384]{3,2,1,0:T(8,128)(2,1)S(1)}, u32[]{:S(2)}, u32[]{:S(2)}) %collective-permute-start.15) | collective-permute-done | bytes 2359328 | tf_op jit(solution)/shard_map/ppermute | solution.py:49
  550.3 17.1 %collective-permute-done.18 = bf16[2,768,384]{2,1,0:T(8,128)(2,1)S(1)} collective-permute-done((bf16[2,768,384]{2,1,0:T(8,128)(2,1)}, bf16[2,768,384]{2,1,0:T(8,128)(2,1)S(1)}, u32[]{:S(2)}, u32[]{:S(2)}) %collective-permute-start.18) | collective-permute-done | bytes 1179680 | tf_op jit(solution)/shard_map/ppermute | solution.py:49
  630.6 11.1 %collective-permute-start.12 = (bf16[256,1536]{1,0:T(8,128)(2,1)}, bf16[256,1536]{1,0:T(8,128)(2,1)}, u32[]{:S(2)}, u32[]{:S(2)}) collective-permute-start(bf16[256,1536]{1,0:T(8,128)(2,1)} %get-tuple-element.85), channel_id=1, source_target_pairs={{0,0},{1,2},{2,1},{3,3},{4,4},{5,6},{6,5},{7,7},{8,8},{9,10},{10,9... | collective-permute-start | bytes 2359304 | tf_op jit(solution)/shard_map/ppermute | solution.py:204
  641.7 16.5 %collective-permute-done.12 = bf16[256,1536]{1,0:T(8,128)(2,1)} collective-permute-done((bf16[256,1536]{1,0:T(8,128)(2,1)}, bf16[256,1536]{1,0:T(8,128)(2,1)}, u32[]{:S(2)}, u32[]{:S(2)}) %collective-permute-start.12) | collective-permute-done | bytes 786464 | tf_op jit(solution)/shard_map/ppermute | solution.py:204
  664.1 8.4 %collective-permute-done.33 = bf16[384,768]{1,0:T(8,128)(2,1)S(1)} collective-permute-done((bf16[384,768]{1,0:T(8,128)(2,1)S(1)}, bf16[384,768]{1,0:T(8,128)(2,1)S(1)}, u32[]{:S(2)}, u32[]{:S(2)}) %collective-permute-start.33) | collective-permute-done | bytes 589856 | tf_op jit(solution)/shard_map/ppermute | solution.py:49
  (407 shorter events, 326.0 us)
Async XLA Ops:
  1.8 39.2 %collective-permute-start.2 = (bf16[576,768]{1,0:T(8,128)(2,1)S(1)}, bf16[576,768]{1,0:T(8,128)(2,1)S(1)}, u32[]{:S(2)}, u32[]{:S(2)}) collective-permute-start(bf16[576,768]{1,0:T(8,128)(2,1)S(1)} %pad_maximum_fusion.6), channel_id=1, source_target_pairs={{0,6},{2,4},{4,2},{6,0},{1,7},{3,5},{5,3},{7,1},{8,14},{10,12},{12... | collective-permute-start | bytes 2654216 | tf_op jit(solution)/shard_map/ppermute | solution.py:121
  9.0 36.5 %collective-permute-start.1 = (bf16[256,1536]{1,0:T(8,128)(2,1)}, bf16[256,1536]{1,0:T(8,128)(2,1)}, u32[]{:S(2)}, u32[]{:S(2)}) collective-permute-start(bf16[256,1536]{1,0:T(8,128)(2,1)} %get-tuple-element.88), channel_id=1, source_target_pairs={{0,2},{1,0},{2,3},{3,1},{4,6},{5,4},{6,7},{7,5},{8,10},{9,8},{10,1... | collective-permute-start | bytes 2359304 | tf_op jit(solution)/shard_map/ppermute | solution.py:194
  9.9 35.6 %collective-permute-start = (bf16[256,1536]{1,0:T(8,128)(2,1)}, bf16[256,1536]{1,0:T(8,128)(2,1)}, u32[]{:S(2)}, u32[]{:S(2)}) collective-permute-start(bf16[256,1536]{1,0:T(8,128)(2,1)} %get-tuple-element.87), channel_id=1, source_target_pairs={{0,0},{1,2},{2,1},{3,3},{4,4},{5,6},{6,5},{7,7},{8,8},{9,10},{10,9... | collective-permute-start | bytes 2359304 | tf_op jit(solution)/shard_map/ppermute | solution.py:193
  63.7 24.3 %collective-permute-start.5 = (bf16[624,768]{1,0:T(8,128)(2,1)S(1)}, bf16[624,768]{1,0:T(8,128)(2,1)}, u32[]{:S(2)}, u32[]{:S(2)}) collective-permute-start(bf16[624,768]{1,0:T(8,128)(2,1)S(1)} %fusion.58), channel_id=1, source_target_pairs={{0,6},{2,4},{4,2},{6,0},{1,7},{3,5},{5,3},{7,1},{8,14},{10,12},{12... | collective-permute-start | bytes 2875400 | tf_op jit(solution)/shard_map/ppermute | solution.py:121
  87.9 27.0 %collective-permute-start.6 = (bf16[624,768]{1,0:T(8,128)(2,1)}, bf16[624,768]{1,0:T(8,128)(2,1)}, u32[]{:S(2)}, u32[]{:S(2)}) collective-permute-start(bf16[624,768]{1,0:T(8,128)(2,1)} %collective-permute-done.5), channel_id=1, source_target_pairs={{0,32},{32,64},{64,96},{96,0},{1,33},{33,65},{65,97},{97,1},{2,34}... | collective-permute-start | bytes 2875400 | tf_op jit(solution)/shard_map/ppermute | solution.py:49
  89.5 22.0 %collective-permute-start.7 = (bf16[624,768]{1,0:T(8,128)(2,1)}, bf16[624,768]{1,0:T(8,128)(2,1)}, u32[]{:S(2)}, u32[]{:S(2)}) collective-permute-start(bf16[624,768]{1,0:T(8,128)(2,1)} %collective-permute-done.5), channel_id=1, source_target_pairs={{0,96},{32,0},{64,32},{96,64},{1,97},{33,1},{65,33},{97,65},{2,98}... | collective-permute-start | bytes 2875400 | tf_op jit(solution)/shard_map/ppermute | solution.py:49
  95.7 38.2 %collective-permute-start.4 = (bf16[512,1536]{1,0:T(8,128)(2,1)S(1)}, bf16[512,1536]{1,0:T(8,128)(2,1)S(1)}, u32[]{:S(2)}, u32[]{:S(2)}) collective-permute-start(bf16[512,1536]{1,0:T(8,128)(2,1)S(1)} %pad_maximum_fusion.4), channel_id=1, source_target_pairs={{0,1},{1,0},{2,3},{3,2},{4,5},{5,4},{6,7},{7,6},{8,9},{9,8},{10,11... | collective-permute-start | bytes 4718600 | tf_op jit(solution)/shard_map/ppermute | solution.py:240
  112.5 11.6 %collective-permute-start.9 = (bf16[312,768]{1,0:T(8,128)(2,1)S(1)}, bf16[312,768]{1,0:T(8,128)(2,1)S(1)}, u32[]{:S(2)}, u32[]{:S(2)}) collective-permute-start(bf16[312,768]{1,0:T(8,128)(2,1)S(1)} %slice.381), channel_id=1, source_target_pairs={{0,96},{32,0},{64,32},{96,64},{1,97},{33,1},{65,33},{97,65},{2,98}... | collective-permute-start | bytes 1437704 | tf_op jit(solution)/shard_map/ppermute | solution.py:49
  130.7 69.0 %collective-permute-start.10 = (bf16[4992,768]{1,0:T(8,128)(2,1)}, bf16[4992,768]{1,0:T(8,128)(2,1)}, u32[]{:S(2)}, u32[]{:S(2)}) collective-permute-start(bf16[4992,768]{1,0:T(8,128)(2,1)} %constant_dynamic-update-slice_fusion.2), channel_id=1, source_target_pairs={{0,1},{1,0},{2,3},{3,2},{4,5},{5,4},{6,7},{7,6},{8,9},{9,8},{10,11... | collective-permute-start | bytes 23003144 | tf_op jit(solution)/shard_map/ppermute | solution.py:125
  321.0 81.7 %collective-permute-start.11 = (f32[512,1536]{0,1:T(8,128)}, f32[512,1536]{0,1:T(8,128)}, u32[]{:S(2)}, u32[]{:S(2)}) collective-permute-start(f32[512,1536]{0,1:T(8,128)} %broadcast_select_fusion), channel_id=1, source_target_pairs={{0,1},{1,0},{2,3},{3,2},{4,5},{5,4},{6,7},{7,6},{8,9},{9,8},{10,11... | collective-permute-start | bytes 9437192 | tf_op jit(solution)/shard_map/ppermute | solution.py:349
  438.2 18.5 %collective-permute-start.14 = (bf16[6144,768]{1,0:T(8,128)(2,1)}, bf16[6144,768]{1,0:T(8,128)(2,1)}, u32[]{:S(2)}, u32[]{:S(2)}) collective-permute-start(bf16[6144,768]{1,0:T(8,128)(2,1)} %fusion.47), channel_id=1, source_target_pairs={{0,1},{1,0},{2,3},{3,2},{4,5},{5,4},{6,7},{7,6},{8,9},{9,8},{10,11... | collective-permute-start | bytes 28311560 | tf_op jit(solution)/shard_map/ppermute | solution.py:125
  484.4 53.7 %collective-permute-start.15 = (bf16[2,2,768,384]{3,2,1,0:T(8,128)(2,1)S(1)}, bf16[2,2,768,384]{3,2,1,0:T(8,128)(2,1)S(1)}, u32[]{:S(2)}, u32[]{:S(2)}) collective-permute-start(bf16[2,2,768,384]{3,2,1,0:T(8,128)(2,1)S(1)} %pad_maximum_fusion.1), channel_id=1, source_target_pairs={{0,32},{32,64},{64,96},{96,0},{1,33},{33,65},{65,97},{97,1},{2,34}... | collective-permute-start | bytes 7077896 | tf_op jit(solution)/shard_map/ppermute | solution.py:49
  484.9 54.9 %collective-permute-start.16 = (bf16[2,2,768,384]{3,2,1,0:T(8,128)(2,1)S(1)}, bf16[2,2,768,384]{3,2,1,0:T(8,128)(2,1)S(1)}, u32[]{:S(2)}, u32[]{:S(2)}) collective-permute-start(bf16[2,2,768,384]{3,2,1,0:T(8,128)(2,1)S(1)} %pad_maximum_fusion.2), channel_id=1, source_target_pairs={{0,96},{32,0},{64,32},{96,64},{1,97},{33,1},{65,33},{97,65},{2,98}... | collective-permute-start | bytes 7077896 | tf_op jit(solution)/shard_map/ppermute | solution.py:49
  539.8 27.6 %collective-permute-start.18 = (bf16[2,768,384]{2,1,0:T(8,128)(2,1)}, bf16[2,768,384]{2,1,0:T(8,128)(2,1)S(1)}, u32[]{:S(2)}, u32[]{:S(2)}) collective-permute-start(bf16[2,768,384]{2,1,0:T(8,128)(2,1)} %fusion.32), channel_id=1, source_target_pairs={{0,32},{32,64},{64,96},{96,0},{1,33},{33,65},{65,97},{97,1},{2,34}... | collective-permute-start | bytes 3538952 | tf_op jit(solution)/shard_map/ppermute | solution.py:49
  541.6 26.7 %collective-permute-start.17 = (bf16[2,768,384]{2,1,0:T(8,128)(2,1)}, bf16[2,768,384]{2,1,0:T(8,128)(2,1)}, u32[]{:S(2)}, u32[]{:S(2)}) collective-permute-start(bf16[2,768,384]{2,1,0:T(8,128)(2,1)} %fusion.34), channel_id=1, source_target_pairs={{0,96},{32,0},{64,32},{96,64},{1,97},{33,1},{65,33},{97,65},{2,98}... | collective-permute-start | bytes 3538952 | tf_op jit(solution)/shard_map/ppermute | solution.py:49
  570.9 14.2 %collective-permute-start.20 = (bf16[2,2,192,384]{3,2,1,0:T(8,128)(2,1)S(1)}, bf16[2,2,192,384]{3,2,1,0:T(8,128)(2,1)S(1)}, u32[]{:S(2)}, u32[]{:S(2)}) collective-permute-start(bf16[2,2,192,384]{3,2,1,0:T(8,128)(2,1)S(1)} %pad_maximum_fusion.12), channel_id=1, source_target_pairs={{0,24},{8,0},{16,8},{24,16},{1,25},{9,1},{17,9},{25,17},{2,26},{10... | collective-permute-start | bytes 1769480 | tf_op jit(solution)/shard_map/ppermute | solution.py:49
  575.0 13.6 %collective-permute-start.19 = (bf16[2,2,192,384]{3,2,1,0:T(8,128)(2,1)S(1)}, bf16[2,2,192,384]{3,2,1,0:T(8,128)(2,1)S(1)}, u32[]{:S(2)}, u32[]{:S(2)}) collective-permute-start(bf16[2,2,192,384]{3,2,1,0:T(8,128)(2,1)S(1)} %pad_maximum_fusion.11), channel_id=1, source_target_pairs={{0,8},{8,16},{16,24},{24,0},{1,9},{9,17},{17,25},{25,1},{2,10},{10... | collective-permute-start | bytes 1769480 | tf_op jit(solution)/shard_map/ppermute | solution.py:49
  596.2 14.2 %collective-permute-start.24 = (bf16[192,768]{1,0:T(8,128)(2,1)S(1)}, bf16[192,768]{1,0:T(8,128)(2,1)S(1)}, u32[]{:S(2)}, u32[]{:S(2)}) collective-permute-start(bf16[192,768]{1,0:T(8,128)(2,1)S(1)} %get-tuple-element.100), channel_id=1, source_target_pairs={{0,6},{2,4},{4,2},{6,0},{1,7},{3,5},{5,3},{7,1},{8,14},{10,12},{12... | collective-permute-start | bytes 884744 | tf_op jit(solution)/shard_map/ppermute | solution.py:121
  598.5 11.9 %collective-permute-start.23 = (bf16[192,768]{1,0:T(8,128)(2,1)S(1)}, bf16[192,768]{1,0:T(8,128)(2,1)S(1)}, u32[]{:S(2)}, u32[]{:S(2)}) collective-permute-start(bf16[192,768]{1,0:T(8,128)(2,1)S(1)} %get-tuple-element.99), channel_id=1, source_target_pairs={{0,4},{4,0},{1,5},{5,1},{2,6},{6,2},{3,7},{7,3},{8,12},{12,8},{9,1... | collective-permute-start | bytes 884744 | tf_op jit(solution)/shard_map/ppermute | solution.py:175
  625.6 36.5 %collective-permute-start.30 = (bf16[768,768]{1,0:T(8,128)(2,1)S(1)}, bf16[768,768]{1,0:T(8,128)(2,1)S(1)}, u32[]{:S(2)}, u32[]{:S(2)}) collective-permute-start(bf16[768,768]{1,0:T(8,128)(2,1)S(1)} %maximum_dynamic-update-slice_fusion.2), channel_id=1, source_target_pairs={{0,32},{32,64},{64,96},{96,0},{1,33},{33,65},{65,97},{97,1},{2,34}... | collective-permute-start | bytes 3538952 | tf_op jit(solution)/shard_map/ppermute | solution.py:49
  625.9 34.4 %collective-permute-start.31 = (bf16[768,768]{1,0:T(8,128)(2,1)S(1)}, bf16[768,768]{1,0:T(8,128)(2,1)S(1)}, u32[]{:S(2)}, u32[]{:S(2)}) collective-permute-start(bf16[768,768]{1,0:T(8,128)(2,1)S(1)} %maximum_dynamic-update-slice_fusion.2), channel_id=1, source_target_pairs={{0,96},{32,0},{64,32},{96,64},{1,97},{33,1},{65,33},{97,65},{2,98}... | collective-permute-start | bytes 3538952 | tf_op jit(solution)/shard_map/ppermute | solution.py:49
  630.6 27.6 %collective-permute-start.12 = (bf16[256,1536]{1,0:T(8,128)(2,1)}, bf16[256,1536]{1,0:T(8,128)(2,1)}, u32[]{:S(2)}, u32[]{:S(2)}) collective-permute-start(bf16[256,1536]{1,0:T(8,128)(2,1)} %get-tuple-element.85), channel_id=1, source_target_pairs={{0,0},{1,2},{2,1},{3,3},{4,4},{5,6},{6,5},{7,7},{8,8},{9,10},{10,9... | collective-permute-start | bytes 2359304 | tf_op jit(solution)/shard_map/ppermute | solution.py:204
  660.4 12.1 %collective-permute-start.33 = (bf16[384,768]{1,0:T(8,128)(2,1)S(1)}, bf16[384,768]{1,0:T(8,128)(2,1)S(1)}, u32[]{:S(2)}, u32[]{:S(2)}) collective-permute-start(bf16[384,768]{1,0:T(8,128)(2,1)S(1)} %slice.436), channel_id=1, source_target_pairs={{0,96},{32,0},{64,32},{96,64},{1,97},{33,1},{65,33},{97,65},{2,98}... | collective-permute-start | bytes 1769480 | tf_op jit(solution)/shard_map/ppermute | solution.py:49
  662.1 13.9 %collective-permute-start.32 = (bf16[384,768]{1,0:T(8,128)(2,1)S(1)}, bf16[384,768]{1,0:T(8,128)(2,1)S(1)}, u32[]{:S(2)}, u32[]{:S(2)}) collective-permute-start(bf16[384,768]{1,0:T(8,128)(2,1)S(1)} %slice.435), channel_id=1, source_target_pairs={{0,32},{32,64},{64,96},{96,0},{1,33},{33,65},{65,97},{97,1},{2,34}... | collective-permute-start | bytes 1769480 | tf_op jit(solution)/shard_map/ppermute | solution.py:49
  (99 other events, 1299.7 us)
